TPU v7x, 512 devices: a whole 4x8x8 slice. The times are simulated.
512 devices in a mesh: seq: 64 (over y, x, core), head: 8 (over z).
Axes of the slice: x: 4, y: 8, z: 8, core: 2. Of those that a mesh axis runs over, the one named last changes fastest.
Arguments:
- queries: bfloat16 [8192, 4096], P('seq', 'head'), may hold values from -0.71875 to 0.71875
- key_rows: bfloat16 [8192, 4096], P('seq', 'head'), may hold values from -0.71875 to 0.71875
- value_rows: bfloat16 [8192, 4096], P('seq', 'head'), may hold values from -0.71875 to 0.71875
- segment_ids: int32 [8192], P('seq'), may hold values from 0 to 7, never falling along the last dimension, each value on 1 to 2048 neighbouring positions
- decay_span: float32 [32], P('head'), may hold values from 30 to 81920, as said below
- norm_gain: float32 [4096], P('head'), may hold values from 0.5 to 1.5
- out_grad: bfloat16 [8192, 4096], P('seq', 'head'), may hold values from -0.71875 to 0.71875
Outputs:
- query_grad: bfloat16 [8192, 4096], P('seq', 'head')
- key_grad: bfloat16 [8192, 4096], P('seq', 'head')
- value_grad: bfloat16 [8192, 4096], P('seq', 'head')
- gain_grad: float32 [4096], P('head')
Inputs may be any that keep to these rules, and one draw needn't show every extreme that they name: segment_ids never falls along the segment; every document of the 8 has a token and the longest has 2048. The decay per token of head h is exp(-1 / decay_span[h]).
All inputs are finite; a program needn't handle non-finite values.
Results may differ from a plain program's by a relative error of at most 0.0012.
Values sent between devices are 32-bit elements; how exact they have to be, the bound alone decides.
A program may use at most 64 MiB of HBM per device.

v0:
```python
import jax
import jax.numpy as jnp
from jax import lax
from jax.sharding import PartitionSpec as P

HEADS = 32
HEAD_DIM = 128


exact = lax.Precision.HIGHEST


def prefix_2(part, axis, combine, identity, reverse):
    count = lax.axis_size(axis)
    place = lax.axis_index(axis)
    ahead = count - 1 - place if reverse else place
    gathered = jax.tree.map(lambda a: lax.all_gather(a, axis), part)
    state = jax.tree.map(lambda a, e: jnp.zeros_like(a) + jnp.asarray(e, a.dtype), part, identity)

    def one(step, state):
        source = count - 1 - step if reverse else step
        return combine(
            state, jax.tree.map(lambda a: lax.dynamic_index_in_dim(a, source, 0, False), gathered)
        )

    return lax.fori_loop(0, ahead, one, state)


def combine_forward(earlier, later):
    state_early, decay_early, first_early, last_early = earlier
    state_late, decay_late, first_late, last_late = later
    passes = jnp.logical_or(
        jnp.logical_and(first_late == last_late, first_late == last_early), first_late < 0
    )
    factor = jnp.where(passes, decay_late, 0.0)
    return (
        state_late + factor[:, None, None] * state_early,
        decay_early * decay_late,
        jnp.where(first_early < 0, first_late, first_early),
        jnp.where(last_late < 0, last_early, last_late),
    )


def combine_backward(earlier, later):
    state_high, decay_high, first_high, last_high = earlier
    state_low, decay_low, first_low, last_low = later
    passes = jnp.logical_or(
        jnp.logical_and(first_low == last_low, last_low == first_high), first_low < 0
    )
    factor = jnp.where(passes, decay_low, 0.0)
    return (
        state_low + factor[:, None, None] * state_high,
        decay_high * decay_low,
        jnp.where(first_low < 0, first_high, first_low),
        jnp.where(last_high < 0, last_low, last_high),
    )


def local(queries, key_rows, value_rows, segment_ids, decay_span, norm_gain, out_grad):
    tok_rows = queries.shape[0]
    heads_here = decay_span.shape[0]
    all_features = HEADS * HEAD_DIM
    block_rows = min(tok_rows, 512)
    block_count = tok_rows // block_rows
    seg_float = segment_ids.astype(jnp.float32)
    positions = jnp.arange(tok_rows, dtype=jnp.float32)
    first_seg = seg_float[0]
    last_seg = seg_float[-1]
    query_full = queries.reshape(tok_rows, heads_here, HEAD_DIM).astype(jnp.float32)
    key_full = key_rows.reshape(tok_rows, heads_here, HEAD_DIM).astype(jnp.float32)
    value_full = value_rows.reshape(tok_rows, heads_here, HEAD_DIM).astype(jnp.float32)
    shard_decay = jnp.exp(-tok_rows / decay_span)
    tail_on = jnp.where(
        (seg_float == last_seg)[:, None],
        jnp.exp(-(tok_rows - 1.0 - positions)[:, None] / decay_span[None, :]),
        0.0,
    )
    local_state = jnp.einsum(
        "thi,thj->hij", key_full * tail_on[:, :, None], value_full, precision=exact
    )
    summary = (local_state, shard_decay, first_seg, last_seg)
    identity = (
        jnp.zeros_like(local_state),
        jnp.ones_like(decay_span),
        jnp.float32(-1.0),
        jnp.float32(-1.0),
    )
    prefix = prefix_2(summary, "seq", combine_forward, identity, False)
    state_in = prefix[0]
    prev_seg = prefix[3]
    offsets = jnp.arange(block_rows, dtype=jnp.float32)
    offset_gap = offsets[:, None] - offsets[None, :]
    causal = offset_gap >= 0
    decay_tile = jnp.where(
        causal[None], jnp.exp(-jnp.maximum(offset_gap, 0.0)[None] / decay_span[:, None, None]), 0.0
    )
    into_weight = jnp.exp(-(offsets + 1.0)[:, None] / decay_span[None, :])
    tail_weight = jnp.exp(-(block_rows - 1.0 - offsets)[:, None] / decay_span[None, :])
    start_weight = jnp.exp(-offsets[:, None] / decay_span[None, :])
    next_weight = jnp.exp(-(block_rows - offsets)[:, None] / decay_span[None, :])
    whole_weight = jnp.exp(-block_rows / decay_span)
    query_blocks = query_full.reshape(block_count, block_rows, heads_here, HEAD_DIM)
    key_blocks = key_full.reshape(block_count, block_rows, heads_here, HEAD_DIM)
    value_blocks = value_full.reshape(block_count, block_rows, heads_here, HEAD_DIM)
    grad_blocks = out_grad.reshape(block_count, block_rows, heads_here * HEAD_DIM)
    seg_blocks = seg_float.reshape(block_count, block_rows)

    def forward_step(carry, inputs):
        state_now, carry_seg, gain_acc = carry
        query_blk, key_blk, value_blk, dy_blk, seg_blk = inputs
        dy_full = dy_blk.astype(jnp.float32)
        same_doc = (seg_blk[:, None] == seg_blk[None, :]).astype(jnp.float32)
        weights = decay_tile * same_doc[None]
        scores = jnp.einsum("thd,shd->hts", query_blk, key_blk, precision=exact) * weights
        inter_on = jnp.where((seg_blk == carry_seg)[:, None], into_weight, 0.0)
        attended = jnp.einsum("hts,shd->thd", scores, value_blk, precision=exact)
        attended = attended + inter_on[:, :, None] * jnp.einsum(
            "thi,hij->thj", query_blk, state_now, precision=exact
        )
        flat_out = attended.reshape(block_rows, heads_here * HEAD_DIM)
        square_part = jnp.sum(flat_out * flat_out, axis=1)
        cross_part = jnp.sum(dy_full * norm_gain[None, :] * flat_out, axis=1)
        square_total, cross_total = lax.psum((square_part, cross_part), "head")
        inv_scale = lax.rsqrt(square_total / all_features + 1e-06)
        out_back = (
            norm_gain[None, :] * dy_full * inv_scale[:, None]
            - flat_out * (inv_scale * inv_scale * inv_scale * cross_total / all_features)[:, None]
        )
        gain_acc = gain_acc + jnp.sum(dy_full * flat_out * inv_scale[:, None], axis=0)
        back_heads = out_back.reshape(block_rows, heads_here, HEAD_DIM)
        grad_scores = jnp.einsum("thd,shd->hts", back_heads, value_blk, precision=exact) * weights
        query_part = jnp.einsum("hts,shd->thd", grad_scores, key_blk, precision=exact)
        query_part = query_part + inter_on[:, :, None] * jnp.einsum(
            "thj,hij->thi", back_heads, state_now, precision=exact
        )
        tail_blk = jnp.where((seg_blk == seg_blk[-1])[:, None], tail_weight, 0.0)
        passes = jnp.logical_and(seg_blk[0] == seg_blk[-1], seg_blk[0] == carry_seg)
        factor = jnp.where(passes, whole_weight, 0.0)
        new_state = (
            jnp.einsum("thi,thj->hij", key_blk * tail_blk[:, :, None], value_blk, precision=exact)
            + factor[:, None, None] * state_now
        )
        outputs = (
            back_heads,
            query_part.reshape(block_rows, heads_here * HEAD_DIM).astype(jnp.bfloat16),
        )
        return ((new_state, seg_blk[-1], gain_acc), outputs)

    start_carry = (state_in, prev_seg, jnp.zeros((heads_here * HEAD_DIM,), jnp.float32))
    forward_carry, forward_out = lax.scan(
        forward_step, start_carry, (query_blocks, key_blocks, value_blocks, grad_blocks, seg_blocks)
    )
    back_blocks = forward_out[0]
    query_grad = forward_out[1].reshape(tok_rows, heads_here * HEAD_DIM)
    gain_local = forward_carry[2]
    back_all = back_blocks.reshape(tok_rows, heads_here, HEAD_DIM)
    start_on = jnp.where(
        (seg_float == first_seg)[:, None], jnp.exp(-positions[:, None] / decay_span[None, :]), 0.0
    )
    local_grad = jnp.einsum(
        "thi,thj->hij", query_full * start_on[:, :, None], back_all, precision=exact
    )
    back_summary = (local_grad, shard_decay, first_seg, last_seg)
    suffix = prefix_2(back_summary, "seq", combine_backward, identity, True)
    grad_in = suffix[0]
    next_seg = suffix[2]

    def backward_step(carry, inputs):
        grad_state, carry_seg = carry
        query_blk, key_blk, value_blk, back_heads, seg_blk = inputs[:5]
        same_doc = (seg_blk[:, None] == seg_blk[None, :]).astype(jnp.float32)
        weights = decay_tile * same_doc[None]
        scores = jnp.einsum("thd,shd->hts", query_blk, key_blk, precision=exact) * weights
        grad_scores = jnp.einsum("thd,shd->hts", back_heads, value_blk, precision=exact) * weights
        key_part = jnp.einsum("hts,thd->shd", grad_scores, query_blk, precision=exact)
        value_part = jnp.einsum("hts,thd->shd", scores, back_heads, precision=exact)
        back_on = jnp.where((seg_blk == carry_seg)[:, None], next_weight, 0.0)
        key_part = key_part + back_on[:, :, None] * jnp.einsum(
            "hij,shj->shi", grad_state, value_blk, precision=exact
        )
        value_part = value_part + back_on[:, :, None] * jnp.einsum(
            "hij,shi->shj", grad_state, key_blk, precision=exact
        )
        start_blk = jnp.where((seg_blk == seg_blk[0])[:, None], start_weight, 0.0)
        passes = jnp.logical_and(seg_blk[0] == seg_blk[-1], seg_blk[-1] == carry_seg)
        factor = jnp.where(passes, whole_weight, 0.0)
        new_state = (
            jnp.einsum(
                "thi,thj->hij", query_blk * start_blk[:, :, None], back_heads, precision=exact
            )
            + factor[:, None, None] * grad_state
        )
        return (
            (new_state, seg_blk[0]),
            (
                key_part.reshape(block_rows, heads_here * HEAD_DIM).astype(jnp.bfloat16),
                value_part.reshape(block_rows, heads_here * HEAD_DIM).astype(jnp.bfloat16),
            ),
        )

    backward_inputs = (query_blocks, key_blocks, value_blocks, back_blocks, seg_blocks)
    _, (key_grad, value_grad) = lax.scan(
        backward_step, (grad_in, next_seg), backward_inputs, reverse=True
    )
    gain_grad = lax.psum(gain_local, "seq")
    return (
        query_grad,
        key_grad.reshape(tok_rows, heads_here * HEAD_DIM),
        value_grad.reshape(tok_rows, heads_here * HEAD_DIM),
        gain_grad,
    )


def solution(mesh):
    in_specs = (
        P("seq", "head"),
        P("seq", "head"),
        P("seq", "head"),
        P("seq"),
        P("head"),
        P("head"),
        P("seq", "head"),
    )
    out_specs = (P("seq", "head"), P("seq", "head"), P("seq", "head"), P("head"))
    return jax.shard_map(local, mesh=mesh, in_specs=in_specs, out_specs=out_specs, check_vma=False)
```

profile of v0, /device:TPU:64, one launch (start us, length us, event | category | flops | bytes accessed | tf_op | source)
XLA Modules:
  0.0 1051.4 jit_solution(12014305828025439504)
XLA Ops:
  9.0 1.3 dynamic-slice.3
  10.3 1.2 fusion.42
  11.5 2.0 broadcast_compare_fusion.1
  18.4 131.0 %all-reduce.3 = (f32[64]{0:T(128)S(1)}, f32[64]{0:T(128)S(1)}, f32[256]{0:T(256)S(1)}) all-reduce(f32[64]{0:T(128)S(1)} %slice_dynamic-update-slice_fusion, f32[64]{0:T(128)S(1)} %get-tuple-element.353, f32[256]{0:T(256)S(1)} %exponential_dynamic-update-slice_fusion), channel_id=1, replica_groups=mesh['seq'=64,'head'=8] {'seq'}, use_global_device_ids=true, to_apply=%add | all-reduce | flops 384 | bytes 3072
  150.7 1.1 convolution_multiply_fusion.1
  154.1 20.0 %psum.23 = f32[128]{0:T(128)S(1)} all-reduce(f32[128]{0:T(128)S(1)} %get-tuple-element.355), channel_id=1, replica_groups=mesh['seq'=64,'head'=8] {'head'}, use_global_device_ids=true, to_apply=%region_3.4 | all-reduce | flops 128 | bytes 1024 | tf_op jit(solution)/shard_map/while/body/eval_jaxpr/psum | solution.py:123
  175.0 16.9 %psum.24 = f32[128]{0:T(128)S(1)} all-reduce(f32[128]{0:T(128)S(1)} %get-tuple-element.312), channel_id=1, replica_groups=mesh['seq'=64,'head'=8] {'head'}, use_global_device_ids=true, to_apply=%region_5.6 | all-reduce | flops 128 | bytes 1024 | tf_op jit(solution)/shard_map/while/body/eval_jaxpr/psum | solution.py:123
  192.7 1.4 fusion.15
  196.8 503.1 %psum.25 = f32[512]{0:T(512)} all-reduce(f32[512]{0:T(512)S(1)} %bitcast.146), channel_id=1, replica_groups=mesh['seq'=64,'head'=8] {'seq'}, use_global_device_ids=true, to_apply=%region_9.10 | all-reduce | flops 512 | bytes 4096 | tf_op jit(solution)/shard_map/psum | solution.py:205
  700.6 341.5 %while.9 = (s32[]{:T(128)}, f32[4,128,128]{2,1,0:T(8,128)S(1)}, f32[]{:T(128)}, s32[]{:T(128)}, f32[64,4,128,128]{3,2,1,0:T(8,128)}, /*index=5*/f32[64]{0:T(128)...) while((s32[]{:T(128)}, f32[4,128,128]{2,1,0:T(8,128)S(1)}, ...), condition=%wide.region_7.8_spmd, body=%wide.region_6.7_spmd.sunk | while | flops 131088 | bytes 786738 | solution.py:26
  709.8 1.1 bitcast_add_fusion.5
  715.3 1.1 bitcast_add_fusion.5
  726.1 1.1 bitcast_add_fusion.5
  731.5 1.1 bitcast_add_fusion.5
  742.4 1.1 bitcast_add_fusion.5
  747.8 1.1 bitcast_add_fusion.5
  758.6 1.1 bitcast_add_fusion.5
  764.1 1.1 bitcast_add_fusion.5
  780.3 1.1 bitcast_add_fusion.5
  785.7 1.1 bitcast_add_fusion.5
  796.6 1.1 bitcast_add_fusion.5
  802.0 1.1 bitcast_add_fusion.5
  812.8 1.1 bitcast_add_fusion.5
  818.3 1.1 bitcast_add_fusion.5
  829.1 1.1 bitcast_add_fusion.5
  834.5 1.1 bitcast_add_fusion.5
  845.4 1.1 bitcast_add_fusion.5
  850.8 1.1 bitcast_add_fusion.5
  861.6 1.1 bitcast_add_fusion.5
  867.0 1.1 bitcast_add_fusion.5
  883.3 1.1 bitcast_add_fusion.5
  888.7 1.1 bitcast_add_fusion.5
  (285 shorter events, 139.6 us)
Async XLA Ops:
  7.2 7.1 copy-start
  7.2 1035.0 %copy-start.3 = (s32[128]{0:T(128)S(1)}, s32[128]{0:T(128)}, u32[]{:S(2)}) copy-start(s32[128]{0:T(128)} %param.14) | copy-start | bytes 1540
  7.2 1036.2 %copy-start.1 = (bf16[128,512]{1,0:T(8,128)(2,1)S(1)}, bf16[128,512]{1,0:T(8,128)(2,1)}, u32[]{:S(2)}) copy-start(bf16[128,512]{1,0:T(8,128)(2,1)} %param.12) | copy-start | bytes 393220
  7.2 1035.0 %copy-start.2 = (f32[4]{0:T(128)S(1)}, f32[4]{0:T(128)}, u32[]{:S(2)}) copy-start(f32[4]{0:T(128)} %param.15) | copy-start | bytes 52
  7.2 145.1 %all-gather.6.cloned.1.call-start = ((), (), s32[]{:S(2)}) async-start(), calls=%async_computation | async-start | bytes 17039360 | tf_op jit(solution)/shard_map/all_gather | solution.py:17
  15.2 685.4 %all-gather.8.cloned.1.call-start = ((), (), s32[]{:S(2)}) async-start(), calls=%async_computation.1 | async-start | bytes 17039360 | tf_op jit(solution)/shard_map/all_gather | solution.py:17
Sparse Core Ops, SparseCore 0:
  15.3 108.7 all-gather.5
  194.2 470.6 all-gather.7
where the time goes:
time: 1060 us; the launch traced here: 1050 us
  blocking collectives  671 us (63%)
  loops' own time  196 us (18%)
  local copies, waits for them, and re-layouts  87 us (8%)
  other arithmetic  75.2 us (7%)
  between operations  14.9 us (1%)
    psum x1, blocking collectives, local(): gain_grad = lax.psum(gain_local, 'seq')  503 us
    another operation x2, loops' own time, prefix_2(): return lax.fori_loop(0, ahead, one, state)  196 us
    unnamed x1, blocking collectives  131 us
    dynamic_slice x126, local copies, waits for them, and re-layouts, one(): lax.dynamic_index_in_dim(a, source, 0, False)  78.2 us
    add x63, other arithmetic, combine_backward(): state_low + factor[:, None, None] * state_high  66.8 us
    psum x2, blocking collectives, forward_step(): square_total, cross_total = lax.psum((square_part, cross_part), 'head')  36.8 us
  transfers between devices with their start and end apart: 2, of which 0 were waited for; matrix products, arithmetic and copies ran while one was open for 1% of the time, Pallas kernels for 0%

commit v1 on v0

v1 whole, which is shorter than its diff:
```python
import functools

import jax
import jax.numpy as jnp
from jax import lax
from jax.experimental import pallas as pl
from jax.experimental.pallas import tpu as pltpu
from jax.sharding import PartitionSpec as P

DIM = 128
ROW = 8
BLOCK = 128
HALF = 64
MESH = pl.DeviceIdType.MESH
F32 = jnp.float32
BF16 = jnp.bfloat16
ORDER = (4, 3, 5, 2, 6, 1, 7)


def split(x):
    high = x.astype(BF16)
    return high, (x - high.astype(F32)).astype(BF16)


def mm(a, b, ca, cb):
    return lax.dot_general(a, b, (((ca,), (cb,)), ((), ())), preferred_element_type=F32)


def mm_split_left(a, b, ca, cb):
    return mm(a[0], b, ca, cb) + mm(a[1], b, ca, cb)


def mm_split_right(a, b, ca, cb):
    return mm(a, b[0], ca, cb) + mm(a, b[1], ca, cb)


def mm_split_both(a, b, ca, cb):
    return mm(a[0], b[0], ca, cb) + (mm(a[0], b[1], ca, cb) + mm(a[1], b[0], ca, cb))


def kernel(
    rows, zs, heads,
    q_hbm, k_hbm, v_hbm, dy_hbm, seg_ref, span_ref, gain_ref,
    dq_ref, dk_ref, dv_ref, gg_ref,
    q_ref, k_ref, v_ref, dy_ref,
    meta_own, meta, states, gathered, totals, carried, prefixes, state_in,
    z_own, z_all, gr_own, gr_all, gc_own, gc_all,
    att_ref, back_ref, w_ref, dk_acc, dv_acc, qk_ref,
    in_sem, meta_s, meta_r, a2a_s, a2a_r, col_s, col_r, ret_s, ret_r,
    z_s, z_r, gr_s, gr_r, gc_s, gc_r,
):
    me = lax.axis_index("seq")
    z = lax.axis_index("head")
    row = me // ROW
    pos = lax.rem(me, ROW)
    features = float(zs * heads * DIM)

    loads = [
        pltpu.make_async_copy(src, dst, in_sem.at[i])
        for i, (src, dst) in enumerate(
            ((k_hbm, k_ref), (v_hbm, v_ref), (q_hbm, q_ref), (dy_hbm, dy_ref))
        )
    ]
    for copy in loads:
        copy.start()

    def seq_of(r, p):
        return {"seq": r * ROW + p, "head": z}

    row_mates = [lax.rem(pos + s, ROW) for s in ORDER]
    col_mates = [lax.rem(row + s, rows) for s in range(1, rows)]
    z_mates = [lax.rem(z + s, zs) for s in range(1, zs)]
    barrier = pltpu.get_barrier_semaphore()
    for p in row_mates:
        pl.semaphore_signal(barrier, inc=1, device_id=seq_of(row, p), device_id_type=MESH)
    for r in col_mates:
        pl.semaphore_signal(barrier, inc=1, device_id=seq_of(r, pos), device_id_type=MESH)
    for other in z_mates:
        pl.semaphore_signal(
            barrier, inc=1, device_id={"seq": me, "head": other}, device_id_type=MESH
        )

    def remote(src, dst, ss, rs, target):
        return pltpu.make_async_remote_copy(
            src_ref=src, dst_ref=dst, send_sem=ss, recv_sem=rs,
            device_id=target, device_id_type=MESH,
        )

    pending = []

    def send(*args):
        copy = remote(*args)
        copy.start()
        pending.append(copy)

    def arrived(buffer, ss, rs):
        remote(buffer, buffer, ss, rs, seq_of(row, row_mates[0])).wait_recv()

    t_col = lax.broadcasted_iota(jnp.int32, (BLOCK, DIM), 0).astype(F32)
    s_row = lax.broadcasted_iota(jnp.int32, (BLOCK, DIM), 1).astype(F32)
    seg_row = seg_ref[...].astype(F32)
    seg_tile = jnp.broadcast_to(seg_row, (BLOCK, DIM))
    seg_col = seg_tile.T
    first_own = jnp.broadcast_to(seg_row[:, 0:1], (1, DIM))
    last_own = jnp.broadcast_to(seg_row[:, BLOCK - 1:BLOCK], (1, DIM))
    tile_row = lax.broadcasted_iota(jnp.int32, (8, DIM), 0)
    meta_own[...] = jnp.where(tile_row == 0, last_own, first_own)
    meta[pos] = meta_own[...]

    inverse = [1.0 / jnp.full((1, DIM), span_ref[h], F32) for h in range(heads)]
    own_inverse = 1.0 / jnp.full((1, DIM), span_ref[pos // 2], F32)
    lam = jnp.exp(-float(BLOCK) * own_inverse)
    lam_row = jnp.exp(-float(BLOCK * ROW) * own_inverse)

    loads[0].wait()
    loads[1].wait()
    for h in range(heads):
        cut = slice(h * DIM, (h + 1) * DIM)
        tail = jnp.where(seg_col == last_own, jnp.exp((t_col - (BLOCK - 1.0)) * inverse[h]), 0.0)
        local = mm_split_right(
            k_ref[:, cut], split(v_ref[:, cut].astype(F32) * tail), 0, 0
        )
        states[0, 2 * h] = local[:HALF]
        states[0, 2 * h + 1] = local[HALF:]

    pl.semaphore_wait(barrier, len(row_mates) + len(col_mates) + len(z_mates))

    def scatter(side):
        for i, p in enumerate(row_mates):
            send(
                states.at[side, p], gathered.at[side, pos],
                a2a_s.at[side, i], a2a_r.at[side, pos], seq_of(row, p),
            )
        gathered[side, pos] = states[side, pos]

    for i, p in enumerate(row_mates):
        send(meta_own, meta.at[pos], meta_s.at[i], meta_r.at[pos], seq_of(row, p))
    scatter(0)

    def scan_first(side):
        for i, p in enumerate(row_mates):
            arrived(gathered.at[side, p], a2a_s.at[side, i], a2a_r.at[side, p])
        order = list(range(ROW)) if side == 0 else list(range(ROW - 1, -1, -1))
        seg_of = [meta[a, side:side + 1, :] for a in order]
        run = gathered[side, order[0]]
        for n in range(1, ROW):
            run = gathered[side, order[n]] + jnp.where(seg_of[n] == seg_of[n - 1], lam, 0.0) * run
        totals[side, :HALF] = run
        totals[side, HALF:] = jnp.broadcast_to(seg_of[-1], (8, DIM))
        for step in range(2):
            move = step + 1 if side == 0 else rows - step - 1
            send(
                totals.at[side], carried.at[side, step],
                col_s.at[side, step], col_r.at[side, step],
                seq_of(lax.rem(row + move, rows), pos),
            )

    def scan_second(side):
        for step in range(2):
            arrived(carried.at[side, step], col_s.at[side, step], col_r.at[side, step])
        order = list(range(ROW)) if side == 0 else list(range(ROW - 1, -1, -1))
        seg_of = [meta[a, side:side + 1, :] for a in order]
        before = row if side == 0 else rows - 1 - row
        near_seg = carried[side, 0, HALF:HALF + 1]
        far_seg = carried[side, 1, HALF:HALF + 1]
        near_seg = jnp.where(before >= 1, near_seg, -1.0)
        far_on = jnp.where(before >= 2, jnp.where(far_seg == near_seg, lam_row, 0.0), 0.0)
        near_on = jnp.where(before >= 1, 1.0, 0.0)
        run = carried[side, 0, :HALF] * near_on + far_on * carried[side, 1, :HALF]
        prev = near_seg
        for n in range(ROW):
            prefixes[side, order[n]] = run
            if n < ROW - 1:
                run = gathered[side, order[n]] + jnp.where(seg_of[n] == prev, lam, 0.0) * run
                prev = seg_of[n]
        for i, p in enumerate(row_mates):
            send(
                prefixes.at[side, p], state_in.at[side, pos],
                ret_s.at[side, i], ret_r.at[side, pos], seq_of(row, p),
            )
        state_in[side, pos] = prefixes[side, pos]
        return near_seg

    def scan_last(side):
        for i, p in enumerate(row_mates):
            arrived(state_in.at[side, p], ret_s.at[side, i], ret_r.at[side, p])

    loads[2].wait()
    causal = t_col >= s_row
    same = seg_col == seg_tile
    keep = jnp.logical_and(causal, same)
    for h in range(heads):
        cut = slice(h * DIM, (h + 1) * DIM)
        weights = jnp.where(keep, jnp.exp(jnp.minimum(s_row - t_col, 0.0) * inverse[h]), 0.0)
        w_ref[h] = weights
        scores = split(mm(q_ref[:, cut], k_ref[:, cut], 1, 1) * weights)
        qk_ref[h, 0] = scores[0]
        qk_ref[h, 1] = scores[1]
        att_ref[h] = mm_split_left(scores, v_ref[:, cut], 1, 0)

    for i, p in enumerate(row_mates):
        arrived(meta.at[p], meta_s.at[i], meta_r.at[p])
    scan_first(0)
    prev_row_seg = scan_second(0)
    prev_seg = jnp.where(pos == 0, prev_row_seg, meta[lax.rem(pos + ROW - 1, ROW), 0:1, :])
    loads[3].wait()
    scan_last(0)

    into_on = seg_col == prev_seg
    squares = jnp.zeros((BLOCK, DIM), F32)
    crosses = jnp.zeros((BLOCK, DIM), F32)
    for h in range(heads):
        cut = slice(h * DIM, (h + 1) * DIM)
        into = jnp.where(into_on, jnp.exp(-(t_col + 1.0) * inverse[h]), 0.0)
        state = split(state_in[0, 2 * h:2 * h + 2].reshape(DIM, DIM))
        att = att_ref[h] + into * mm_split_right(q_ref[:, cut], state, 1, 0)
        att_ref[h] = att
        squares = squares + att * att
        crosses = crosses + dy_ref[:, cut].astype(F32) * gain_ref[:, cut] * att
    square_row = jnp.sum(squares.T, axis=0, keepdims=True)
    cross_row = jnp.sum(crosses.T, axis=0, keepdims=True)
    z_own[...] = jnp.where(tile_row == 0, square_row, cross_row)
    for i, other in enumerate(z_mates):
        send(z_own, z_all.at[z], z_s.at[i], z_r.at[z], {"seq": me, "head": other})
    z_all[z] = z_own[...]
    for i, other in enumerate(z_mates):
        arrived(z_all.at[other], z_s.at[i], z_r.at[other])
    both = z_all[0]
    for i in range(1, zs):
        both = both + z_all[i]
    inv_row = lax.rsqrt(both[0:1] / features + 1e-06)
    off_row = inv_row * inv_row * inv_row * both[1:2] / features
    inv = jnp.broadcast_to(inv_row, (BLOCK, DIM)).T
    off = jnp.broadcast_to(off_row, (BLOCK, DIM)).T

    for h in range(heads):
        cut = slice(h * DIM, (h + 1) * DIM)
        dy = dy_ref[:, cut].astype(F32)
        att = att_ref[h]
        scaled = dy * inv
        back = gain_ref[:, cut] * scaled - att * off
        back_ref[h] = back
        gr_own[h:h + 1] = jnp.sum(scaled * att, axis=0, keepdims=True)
        start = jnp.where(seg_col == first_own, jnp.exp(-t_col * inverse[h]), 0.0)
        local = mm_split_right(q_ref[:, cut], split(back * start), 0, 0)
        states[1, 2 * h] = local[:HALF]
        states[1, 2 * h + 1] = local[HALF:]
    scatter(1)
    for i, p in enumerate(row_mates):
        send(gr_own, gr_all.at[pos], gr_s.at[i], gr_r.at[pos], seq_of(row, p))
    gr_all[pos] = gr_own[...]

    def inner(h):
        cut = slice(h * DIM, (h + 1) * DIM)
        back = split(back_ref[h])
        weights = w_ref[h]
        grads = split(mm_split_left(back, v_ref[:, cut], 1, 1) * weights)
        into = jnp.where(into_on, jnp.exp(-(t_col + 1.0) * inverse[h]), 0.0)
        state = split(state_in[0, 2 * h:2 * h + 2].reshape(DIM, DIM))
        dq = mm_split_left(grads, k_ref[:, cut], 1, 0) + into * mm_split_both(back, state, 1, 1)
        dq_ref[:, cut] = dq.astype(BF16)
        dk_acc[h] = mm_split_left(grads, q_ref[:, cut], 0, 0)
        dv_acc[h] = mm_split_both((qk_ref[h, 0], qk_ref[h, 1]), back, 0, 0)

    inner(0)
    inner(1)
    scan_first(1)
    for i, p in enumerate(row_mates):
        arrived(gr_all.at[p], gr_s.at[i], gr_r.at[p])
    total = gr_all[0]
    for a in range(1, ROW):
        total = total + gr_all[a]
    gc_own[...] = total
    gc_all[row] = total
    for i, r in enumerate(col_mates):
        send(gc_own, gc_all.at[row], gc_s.at[i], gc_r.at[row], seq_of(r, pos))
    inner(2)
    next_row_seg = scan_second(1)
    next_seg = jnp.where(pos == ROW - 1, next_row_seg, meta[lax.rem(pos + 1, ROW), 1:2, :])
    inner(3)
    for i, r in enumerate(col_mates):
        arrived(gc_all.at[r], gc_s.at[i], gc_r.at[r])
    total = gc_all[0]
    for a in range(1, rows):
        total = total + gc_all[a]
    for h in range(heads):
        gg_ref[:, h * DIM:(h + 1) * DIM] = total[h:h + 1]
    scan_last(1)

    next_on = seg_col == next_seg
    for h in range(heads):
        cut = slice(h * DIM, (h + 1) * DIM)
        weight = jnp.where(next_on, jnp.exp((t_col - float(BLOCK)) * inverse[h]), 0.0)
        grad = split(state_in[1, 2 * h:2 * h + 2].reshape(DIM, DIM))
        dk = dk_acc[h] + weight * mm_split_right(v_ref[:, cut], grad, 1, 1)
        dv = dv_acc[h] + weight * mm_split_right(k_ref[:, cut], grad, 1, 0)
        dk_ref[:, cut] = dk.astype(BF16)
        dv_ref[:, cut] = dv.astype(BF16)
    for copy in pending:
        copy.wait_send()


def local(queries, key_rows, value_rows, segment_ids, decay_span, norm_gain, out_grad):
    rows = lax.axis_size("seq") // ROW
    zs = lax.axis_size("head")
    heads = decay_span.shape[0]
    width = heads * DIM
    whole = pl.BlockSpec(memory_space=pltpu.VMEM)
    far = pl.BlockSpec(memory_space=pl.ANY)
    wide = pltpu.VMEM((BLOCK, width), BF16)
    square = pltpu.VMEM((heads, DIM, DIM), F32)
    dma = pltpu.SemaphoreType.DMA
    out = jax.ShapeDtypeStruct((BLOCK, width), BF16)
    dq, dk, dv, gg = pl.pallas_call(
        functools.partial(kernel, rows, zs, heads),
        out_shape=(out, out, out, jax.ShapeDtypeStruct((1, width), F32)),
        in_specs=[far] * 4 + [whole, pl.BlockSpec(memory_space=pltpu.SMEM), whole],
        out_specs=(whole,) * 4,
        scratch_shapes=[
            wide, wide, wide, wide,
            pltpu.VMEM((8, DIM), F32),
            pltpu.VMEM((ROW, 8, DIM), F32),
            pltpu.VMEM((2, ROW, HALF, DIM), F32),
            pltpu.VMEM((2, ROW, HALF, DIM), F32),
            pltpu.VMEM((2, HALF + 8, DIM), F32),
            pltpu.VMEM((2, 2, HALF + 8, DIM), F32),
            pltpu.VMEM((2, ROW, HALF, DIM), F32),
            pltpu.VMEM((2, ROW, HALF, DIM), F32),
            pltpu.VMEM((8, DIM), F32),
            pltpu.VMEM((zs, 8, DIM), F32),
            pltpu.VMEM((heads, DIM), F32),
            pltpu.VMEM((ROW, heads, DIM), F32),
            pltpu.VMEM((heads, DIM), F32),
            pltpu.VMEM((rows, heads, DIM), F32),
            square, square, square, square, square,
            pltpu.VMEM((heads, 2, DIM, DIM), BF16),
            dma((4,)),
            dma((ROW,)), dma((ROW,)),
            dma((2, ROW)), dma((2, ROW)),
            dma((2, 2)), dma((2, 2)),
            dma((2, ROW)), dma((2, ROW)),
            dma((zs,)), dma((zs,)),
            dma((ROW,)), dma((ROW,)),
            dma((rows,)), dma((rows,)),
        ],
        compiler_params=pltpu.CompilerParams(collective_id=0, has_side_effects=True),
    )(
        queries, key_rows, value_rows, out_grad,
        segment_ids.reshape(1, BLOCK), decay_span, norm_gain.reshape(1, width),
    )
    return dq, dk, dv, gg.reshape(width)


def solution(mesh):
    in_specs = (
        P("seq", "head"),
        P("seq", "head"),
        P("seq", "head"),
        P("seq"),
        P("head"),
        P("head"),
        P("seq", "head"),
    )
    out_specs = (P("seq", "head"), P("seq", "head"), P("seq", "head"), P("head"))
    return jax.shard_map(local, mesh=mesh, in_specs=in_specs, out_specs=out_specs, check_vma=False)
```

time: 1060 us -> 56.3 us (0.05)
  the two profiles are of different devices: /device:TPU:64 before, /device:TPU:1 now
where the time goes in v1:
time: 56.3 us; the launch traced here: 56.1 us
  Pallas kernels  51.6 us (92%)
  local copies, waits for them, and re-layouts  3.81 us (7%)
  between operations  0.65 us (1%)
    pallas_call x1, Pallas kernels, local(): pl.pallas_call(functools.partial(kernel, rows, zs, heads), out_shape=(out...  51.6 us
    unnamed x10, local copies, waits for them, and re-layouts  3.81 us

profile of v1, /device:TPU:1, one launch (start us, length us, event | category | flops | bytes accessed | tf_op | source)
XLA Modules:
  0.0 56.1 jit_solution(5901686142034412849)
XLA Ops:
  0.6 51.6 %shard_map.102 = (bf16[128,512]{1,0:T(8,128)(2,1)}, bf16[128,512]{1,0:T(8,128)(2,1)}, bf16[128,512]{1,0:T(8,128)(2,1)}, f32[1,512]{1,0:T(1,128)}) custom-call(bf16[128,512]{1,0:T(8,128)(2,1)} %q_hbm.1, bf16[128,512]{1,0:T(8,128)(2,1)} %k_hbm.1, bf16[128,512]{1,0:T(8,128)(2,1)} %v_hbm.1, bf16[128,512]{1,0:T(8,128)(2,1)} %dy_hbm.1, s32[1,128]{1,0:T(1,128)} %bitcast.5, ...), custom_call_target="tpu_custom_call" | custom-call | tf_op jit(solution)/shard_map/pallas_call | solution.py:314
  52.3 0.0 copy-start.1
  52.3 1.6 %copy.15 = bf16[128,512]{1,0:T(8,128)(2,1)} copy(bf16[128,512]{1,0:T(8,128)(2,1)} %get-tuple-element.16) | data formatting | bytes 262144
  53.9 0.0 copy-done.1
  53.9 0.0 copy-start
  53.9 0.7 %copy.16 = bf16[128,512]{1,0:T(8,128)(2,1)} copy(bf16[128,512]{1,0:T(8,128)(2,1)S(1)} %copy-done.1) | data formatting | bytes 262144
  54.5 0.3 copy-done
  54.8 0.0 copy-start.2
  54.8 0.7 %copy.17 = bf16[128,512]{1,0:T(8,128)(2,1)} copy(bf16[128,512]{1,0:T(8,128)(2,1)S(1)} %copy-done) | data formatting | bytes 262144
  55.5 0.0 copy-done.2
  55.5 0.6 %copy.18 = f32[512]{0:T(512)} copy(f32[512]{0:T(512)S(1)} %bitcast.4) | data formatting | bytes 4096
Async XLA Ops:
  52.3 1.6 %copy-start.1 = (bf16[128,512]{1,0:T(8,128)(2,1)S(1)}, bf16[128,512]{1,0:T(8,128)(2,1)}, u32[]{:S(2)}) copy-start(bf16[128,512]{1,0:T(8,128)(2,1)} %get-tuple-element.17) | copy-start | bytes 393220
  53.9 1.0 %copy-start = (bf16[128,512]{1,0:T(8,128)(2,1)S(1)}, bf16[128,512]{1,0:T(8,128)(2,1)}, u32[]{:S(2)}) copy-start(bf16[128,512]{1,0:T(8,128)(2,1)} %get-tuple-element.18) | copy-start | bytes 393220
  54.8 0.7 %copy-start.2 = (f32[1,512]{1,0:T(1,128)S(1)}, f32[1,512]{1,0:T(1,128)}, u32[]{:S(2)}) copy-start(f32[1,512]{1,0:T(1,128)} %get-tuple-element.11) | copy-start | bytes 6148

commit v2 on v1

--- a/solution.py
+++ b/solution.py
@@ -11,6 +11,9 @@
 ROW = 8
 BLOCK = 128
 HALF = 64
+CHUNKS = 4
+PART = HALF // CHUNKS
+HEAD_ROWS = 8
 MESH = pl.DeviceIdType.MESH
 F32 = jnp.float32
 BF16 = jnp.bfloat16
@@ -40,9 +43,9 @@
 
 def kernel(
     rows, zs, heads,
-    q_hbm, k_hbm, v_hbm, dy_hbm, seg_ref, span_ref, gain_ref,
+    q_hbm, k_hbm, v_hbm, dy_hbm, seg_hbm, span_hbm, gain_hbm,
     dq_ref, dk_ref, dv_ref, gg_ref,
-    q_ref, k_ref, v_ref, dy_ref,
+    q_ref, k_ref, v_ref, dy_ref, seg_ref, span_ref, gain_ref,
     meta_own, meta, states, gathered, totals, carried, prefixes, state_in,
     z_own, z_all, gr_own, gr_all, gc_own, gc_all,
     att_ref, back_ref, w_ref, dk_acc, dv_acc, qk_ref,
@@ -58,18 +61,21 @@
     loads = [
         pltpu.make_async_copy(src, dst, in_sem.at[i])
         for i, (src, dst) in enumerate(
-            ((k_hbm, k_ref), (v_hbm, v_ref), (q_hbm, q_ref), (dy_hbm, dy_ref))
+            (
+                (k_hbm, k_ref), (v_hbm, v_ref), (q_hbm, q_ref), (dy_hbm, dy_ref),
+                (seg_hbm, seg_ref), (span_hbm, span_ref), (gain_hbm, gain_ref),
+            )
         )
     ]
-    for copy in loads:
-        copy.start()
+    for i in (4, 5, 0, 1, 2, 3, 6):
+        loads[i].start()
 
     def seq_of(r, p):
         return {"seq": r * ROW + p, "head": z}
 
     row_mates = [lax.rem(pos + s, ROW) for s in ORDER]
     col_mates = [lax.rem(row + s, rows) for s in range(1, rows)]
-    z_mates = [lax.rem(z + s, zs) for s in range(1, zs)]
+    z_mates = [lax.rem(z + s, zs) for s in sorted(range(1, zs), key=lambda s: -min(s, zs - s))]
     barrier = pltpu.get_barrier_semaphore()
     for p in row_mates:
         pl.semaphore_signal(barrier, inc=1, device_id=seq_of(row, p), device_id_type=MESH)
@@ -86,15 +92,18 @@
             device_id=target, device_id_type=MESH,
         )
 
-    pending = []
-
     def send(*args):
-        copy = remote(*args)
-        copy.start()
-        pending.append(copy)
-
-    def arrived(buffer, ss, rs):
-        remote(buffer, buffer, ss, rs, seq_of(row, row_mates[0])).wait_recv()
+        remote(*args).start()
+
+    def arrived(buffer, rs):
+        remote(buffer, buffer, rs, rs, seq_of(row, row_mates[0])).wait_recv()
+
+    def sent(buffer, ss):
+        remote(buffer, buffer, ss, ss, seq_of(row, row_mates[0])).wait_send()
+
+    row_others = pl.ds(0, ROW - 1)
+    loads[4].wait()
+    loads[5].wait()
 
     t_col = lax.broadcasted_iota(jnp.int32, (BLOCK, DIM), 0).astype(F32)
     s_row = lax.broadcasted_iota(jnp.int32, (BLOCK, DIM), 1).astype(F32)
@@ -126,64 +135,77 @@
     pl.semaphore_wait(barrier, len(row_mates) + len(col_mates) + len(z_mates))
 
     def scatter(side):
-        for i, p in enumerate(row_mates):
-            send(
-                states.at[side, p], gathered.at[side, pos],
-                a2a_s.at[side, i], a2a_r.at[side, pos], seq_of(row, p),
-            )
+        for c in range(CHUNKS):
+            part = pl.ds(c * PART, PART)
+            for p in row_mates:
+                send(
+                    states.at[side, p, part], gathered.at[side, pos, part],
+                    a2a_s.at[side], a2a_r.at[side, c], seq_of(row, p),
+                )
         gathered[side, pos] = states[side, pos]
 
-    for i, p in enumerate(row_mates):
-        send(meta_own, meta.at[pos], meta_s.at[i], meta_r.at[pos], seq_of(row, p))
+    def piece(c):
+        return pl.ds(HEAD_ROWS + c * PART, PART) if c else pl.ds(0, HEAD_ROWS + PART)
+
+    def order_of(side):
+        order = list(range(ROW)) if side == 0 else list(range(ROW - 1, -1, -1))
+        return order, [meta[a, side:side + 1, :] for a in order]
+
+    for p in row_mates:
+        send(meta_own, meta.at[pos], meta_s.at[0], meta_r.at[0], seq_of(row, p))
     scatter(0)
 
     def scan_first(side):
-        for i, p in enumerate(row_mates):
-            arrived(gathered.at[side, p], a2a_s.at[side, i], a2a_r.at[side, p])
-        order = list(range(ROW)) if side == 0 else list(range(ROW - 1, -1, -1))
-        seg_of = [meta[a, side:side + 1, :] for a in order]
-        run = gathered[side, order[0]]
-        for n in range(1, ROW):
-            run = gathered[side, order[n]] + jnp.where(seg_of[n] == seg_of[n - 1], lam, 0.0) * run
-        totals[side, :HALF] = run
-        totals[side, HALF:] = jnp.broadcast_to(seg_of[-1], (8, DIM))
-        for step in range(2):
-            move = step + 1 if side == 0 else rows - step - 1
-            send(
-                totals.at[side], carried.at[side, step],
-                col_s.at[side, step], col_r.at[side, step],
-                seq_of(lax.rem(row + move, rows), pos),
-            )
+        order, seg_of = order_of(side)
+        factor = [jnp.where(seg_of[n] == seg_of[n - 1], lam, 0.0) for n in range(1, ROW)]
+        for c in range(CHUNKS):
+            part = pl.ds(c * PART, PART)
+            arrived(gathered.at[side, row_others, part], a2a_r.at[side, c])
+            run = gathered[side, order[0], part]
+            for n in range(1, ROW):
+                run = gathered[side, order[n], part] + factor[n - 1] * run
+            if c == 0:
+                totals[side, :HEAD_ROWS] = jnp.broadcast_to(seg_of[-1], (HEAD_ROWS, DIM))
+            totals[side, pl.ds(HEAD_ROWS + c * PART, PART)] = run
+            for step in (1, 0):
+                move = step + 1 if side == 0 else rows - step - 1
+                send(
+                    totals.at[side, piece(c)], carried.at[side, step, piece(c)],
+                    col_s.at[side], col_r.at[side, step, c],
+                    seq_of(lax.rem(row + move, rows), pos),
+                )
 
     def scan_second(side):
-        for step in range(2):
-            arrived(carried.at[side, step], col_s.at[side, step], col_r.at[side, step])
-        order = list(range(ROW)) if side == 0 else list(range(ROW - 1, -1, -1))
-        seg_of = [meta[a, side:side + 1, :] for a in order]
+        order, seg_of = order_of(side)
         before = row if side == 0 else rows - 1 - row
-        near_seg = carried[side, 0, HALF:HALF + 1]
-        far_seg = carried[side, 1, HALF:HALF + 1]
-        near_seg = jnp.where(before >= 1, near_seg, -1.0)
-        far_on = jnp.where(before >= 2, jnp.where(far_seg == near_seg, lam_row, 0.0), 0.0)
         near_on = jnp.where(before >= 1, 1.0, 0.0)
-        run = carried[side, 0, :HALF] * near_on + far_on * carried[side, 1, :HALF]
-        prev = near_seg
-        for n in range(ROW):
-            prefixes[side, order[n]] = run
-            if n < ROW - 1:
-                run = gathered[side, order[n]] + jnp.where(seg_of[n] == prev, lam, 0.0) * run
-                prev = seg_of[n]
-        for i, p in enumerate(row_mates):
-            send(
-                prefixes.at[side, p], state_in.at[side, pos],
-                ret_s.at[side, i], ret_r.at[side, pos], seq_of(row, p),
-            )
+        for c in range(CHUNKS):
+            for step in range(2):
+                arrived(carried.at[side, step, piece(c)], col_r.at[side, step, c])
+            if c == 0:
+                near_seg = carried[side, 0, 0:1]
+                far_seg = carried[side, 1, 0:1]
+                near_seg = jnp.where(before >= 1, near_seg, -1.0)
+                far_on = jnp.where(before >= 2, jnp.where(far_seg == near_seg, lam_row, 0.0), 0.0)
+                prev = [near_seg] + seg_of[:-1]
+                factor = [jnp.where(a == b, lam, 0.0) for a, b in zip(seg_of, prev)]
+            rows_c = pl.ds(HEAD_ROWS + c * PART, PART)
+            part = pl.ds(c * PART, PART)
+            run = carried[side, 0, rows_c] * near_on + far_on * carried[side, 1, rows_c]
+            for n in range(ROW):
+                prefixes[side, order[n], part] = run
+                if n < ROW - 1:
+                    run = gathered[side, order[n], part] + factor[n] * run
+            for p in row_mates:
+                send(
+                    prefixes.at[side, p, part], state_in.at[side, pos, part],
+                    ret_s.at[side], ret_r.at[side], seq_of(row, p),
+                )
         state_in[side, pos] = prefixes[side, pos]
         return near_seg
 
     def scan_last(side):
-        for i, p in enumerate(row_mates):
-            arrived(state_in.at[side, p], ret_s.at[side, i], ret_r.at[side, p])
+        arrived(state_in.at[side, row_others], ret_r.at[side])
 
     loads[2].wait()
     causal = t_col >= s_row
@@ -198,12 +220,12 @@
         qk_ref[h, 1] = scores[1]
         att_ref[h] = mm_split_left(scores, v_ref[:, cut], 1, 0)
 
-    for i, p in enumerate(row_mates):
-        arrived(meta.at[p], meta_s.at[i], meta_r.at[p])
+    arrived(meta.at[row_others], meta_r.at[0])
     scan_first(0)
     prev_row_seg = scan_second(0)
     prev_seg = jnp.where(pos == 0, prev_row_seg, meta[lax.rem(pos + ROW - 1, ROW), 0:1, :])
     loads[3].wait()
+    loads[6].wait()
     scan_last(0)
 
     into_on = seg_col == prev_seg
@@ -219,12 +241,13 @@
         crosses = crosses + dy_ref[:, cut].astype(F32) * gain_ref[:, cut] * att
     square_row = jnp.sum(squares.T, axis=0, keepdims=True)
     cross_row = jnp.sum(crosses.T, axis=0, keepdims=True)
-    z_own[...] = jnp.where(tile_row == 0, square_row, cross_row)
-    for i, other in enumerate(z_mates):
-        send(z_own, z_all.at[z], z_s.at[i], z_r.at[z], {"seq": me, "head": other})
+    z_own[0:1] = square_row
+    z_own[1:2] = cross_row
+    for other in z_mates:
+        send(z_own, z_all.at[z], z_s.at[0], z_r.at[0], {"seq": me, "head": other})
     z_all[z] = z_own[...]
-    for i, other in enumerate(z_mates):
-        arrived(z_all.at[other], z_s.at[i], z_r.at[other])
+    if zs > 1:
+        arrived(z_all.at[pl.ds(0, zs - 1)], z_r.at[0])
     both = z_all[0]
     for i in range(1, zs):
         both = both + z_all[i]
@@ -246,8 +269,8 @@
         states[1, 2 * h] = local[:HALF]
         states[1, 2 * h + 1] = local[HALF:]
     scatter(1)
-    for i, p in enumerate(row_mates):
-        send(gr_own, gr_all.at[pos], gr_s.at[i], gr_r.at[pos], seq_of(row, p))
+    for p in row_mates:
+        send(gr_own, gr_all.at[pos], gr_s.at[0], gr_r.at[0], seq_of(row, p))
     gr_all[pos] = gr_own[...]
 
     def inner(h):
@@ -265,21 +288,19 @@
     inner(0)
     inner(1)
     scan_first(1)
-    for i, p in enumerate(row_mates):
-        arrived(gr_all.at[p], gr_s.at[i], gr_r.at[p])
+    arrived(gr_all.at[row_others], gr_r.at[0])
     total = gr_all[0]
     for a in range(1, ROW):
         total = total + gr_all[a]
     gc_own[...] = total
     gc_all[row] = total
-    for i, r in enumerate(col_mates):
-        send(gc_own, gc_all.at[row], gc_s.at[i], gc_r.at[row], seq_of(r, pos))
+    for r in col_mates:
+        send(gc_own, gc_all.at[row], gc_s.at[0], gc_r.at[0], seq_of(r, pos))
     inner(2)
     next_row_seg = scan_second(1)
     next_seg = jnp.where(pos == ROW - 1, next_row_seg, meta[lax.rem(pos + 1, ROW), 1:2, :])
     inner(3)
-    for i, r in enumerate(col_mates):
-        arrived(gc_all.at[r], gc_s.at[i], gc_r.at[r])
+    arrived(gc_all.at[pl.ds(0, rows - 1)], gc_r.at[0])
     total = gc_all[0]
     for a in range(1, rows):
         total = total + gc_all[a]
@@ -296,8 +317,26 @@
         dv = dv_acc[h] + weight * mm_split_right(k_ref[:, cut], grad, 1, 0)
         dk_ref[:, cut] = dk.astype(BF16)
         dv_ref[:, cut] = dv.astype(BF16)
-    for copy in pending:
-        copy.wait_send()
+    sent(meta.at[row_others], meta_s.at[0])
+    for side in range(2):
+        sent(states.at[side, row_others], a2a_s.at[side])
+        sent(carried.at[side], col_s.at[side])
+        sent(prefixes.at[side, row_others], ret_s.at[side])
+    if zs > 1:
+        sent(z_all.at[pl.ds(0, zs - 1)], z_s.at[0])
+    sent(gr_all.at[row_others], gr_s.at[0])
+    sent(gc_all.at[pl.ds(0, rows - 1)], gc_s.at[0])
+
+
+def store(*refs):
+    count = (len(refs) - 1) // 2
+    copies = [
+        pltpu.make_async_copy(refs[i], refs[count + i], refs[-1].at[i]) for i in range(count)
+    ]
+    for copy in copies:
+        copy.start()
+    for copy in copies:
+        copy.wait()
 
 
 def local(queries, key_rows, value_rows, segment_ids, decay_span, norm_gain, out_grad):
@@ -305,49 +344,59 @@
     zs = lax.axis_size("head")
     heads = decay_span.shape[0]
     width = heads * DIM
-    whole = pl.BlockSpec(memory_space=pltpu.VMEM)
     far = pl.BlockSpec(memory_space=pl.ANY)
+    near = pl.BlockSpec(memory_space=pltpu.VMEM)
     wide = pltpu.VMEM((BLOCK, width), BF16)
     square = pltpu.VMEM((heads, DIM, DIM), F32)
+    pieces = pltpu.VMEM((2, ROW, HALF, DIM), F32)
     dma = pltpu.SemaphoreType.DMA
-    out = jax.ShapeDtypeStruct((BLOCK, width), BF16)
-    dq, dk, dv, gg = pl.pallas_call(
+    kept = pltpu.VMEM((1, width), F32)
+    results = pl.pallas_call(
         functools.partial(kernel, rows, zs, heads),
-        out_shape=(out, out, out, jax.ShapeDtypeStruct((1, width), F32)),
-        in_specs=[far] * 4 + [whole, pl.BlockSpec(memory_space=pltpu.SMEM), whole],
-        out_specs=(whole,) * 4,
+        out_shape=(wide, wide, wide, kept),
+        in_specs=[far] * 7,
+        out_specs=(near,) * 4,
         scratch_shapes=[
             wide, wide, wide, wide,
+            pltpu.VMEM((1, BLOCK), jnp.int32), pltpu.SMEM((heads,), F32), kept,
             pltpu.VMEM((8, DIM), F32),
             pltpu.VMEM((ROW, 8, DIM), F32),
-            pltpu.VMEM((2, ROW, HALF, DIM), F32),
-            pltpu.VMEM((2, ROW, HALF, DIM), F32),
-            pltpu.VMEM((2, HALF + 8, DIM), F32),
-            pltpu.VMEM((2, 2, HALF + 8, DIM), F32),
-            pltpu.VMEM((2, ROW, HALF, DIM), F32),
-            pltpu.VMEM((2, ROW, HALF, DIM), F32),
-            pltpu.VMEM((8, DIM), F32),
-            pltpu.VMEM((zs, 8, DIM), F32),
+            pieces,
+            pieces,
+            pltpu.VMEM((2, HEAD_ROWS + HALF, DIM), F32),
+            pltpu.VMEM((2, 2, HEAD_ROWS + HALF, DIM), F32),
+            pieces,
+            pieces,
+            pltpu.VMEM((2, DIM), F32),
+            pltpu.VMEM((zs, 2, DIM), F32),
             pltpu.VMEM((heads, DIM), F32),
             pltpu.VMEM((ROW, heads, DIM), F32),
             pltpu.VMEM((heads, DIM), F32),
             pltpu.VMEM((rows, heads, DIM), F32),
             square, square, square, square, square,
             pltpu.VMEM((heads, 2, DIM, DIM), BF16),
-            dma((4,)),
-            dma((ROW,)), dma((ROW,)),
-            dma((2, ROW)), dma((2, ROW)),
-            dma((2, 2)), dma((2, 2)),
-            dma((2, ROW)), dma((2, ROW)),
-            dma((zs,)), dma((zs,)),
-            dma((ROW,)), dma((ROW,)),
-            dma((rows,)), dma((rows,)),
+            dma((7,)),
+            dma((1,)), dma((1,)),
+            dma((2,)), dma((2, CHUNKS)),
+            dma((2,)), dma((2, 2, CHUNKS)),
+            dma((2,)), dma((2,)),
+            dma((1,)), dma((1,)),
+            dma((1,)), dma((1,)),
+            dma((1,)), dma((1,)),
         ],
         compiler_params=pltpu.CompilerParams(collective_id=0, has_side_effects=True),
     )(
         queries, key_rows, value_rows, out_grad,
         segment_ids.reshape(1, BLOCK), decay_span, norm_gain.reshape(1, width),
     )
+    out = jax.ShapeDtypeStruct((BLOCK, width), BF16)
+    dq, dk, dv, gg = pl.pallas_call(
+        store,
+        out_shape=(out, out, out, jax.ShapeDtypeStruct((1, width), F32)),
+        in_specs=[near] * 4,
+        out_specs=(far,) * 4,
+        scratch_shapes=[dma((4,))],
+    )(*[pltpu.with_memory_space_constraint(r, pltpu.VMEM) for r in results])
     return dq, dk, dv, gg.reshape(width)
 
 

time: 56.3 us -> 47.1 us (0.84)
  Pallas kernels: 51.6 us -> 46.3 us
  local copies, waits for them, and re-layouts: 3.81 us -> 0 us
    pallas_call x1 -> x2, Pallas kernels: 51.6 us -> 46.3 us  [the longest x1 45.5 us: local(): pl.pallas_call(functools.partial(kernel, rows, zs, heads), out_shape=(wid...]
    unnamed x10 -> x0, local copies, waits for them, and re-layouts: 3.81 us -> none
where the time goes in v2:
time: 47.1 us; the launch traced here: 46.9 us
  Pallas kernels  46.3 us (98%)
  between operations  0.64 us (1%)
    pallas_call x1, Pallas kernels, local(): pl.pallas_call(functools.partial(kernel, rows, zs, heads), out_shape=(wid...  45.5 us

profile of v2, /device:TPU:1, one launch (start us, length us, event | category | flops | bytes accessed | tf_op | source)
XLA Modules:
  0.0 46.9 jit_solution(12057206396937390844)
XLA Ops:
  0.6 45.5 %shard_map.102 = (bf16[128,512]{1,0:T(8,128)(2,1)S(1)}, bf16[128,512]{1,0:T(8,128)(2,1)S(1)}, bf16[128,512]{1,0:T(8,128)(2,1)S(1)}, f32[1,512]{1,0:T(1,128)S(1)}) custom-call(bf16[128,512]{1,0:T(8,128)(2,1)} %q_hbm.1, bf16[128,512]{1,0:T(8,128)(2,1)} %k_hbm.1, bf16[128,512]{1,0:T(8,128)(2,1)} %v_hbm.1, bf16[128,512]{1,0:T(8,128)(2,1)} %dy_hbm.1, ...), custom_call_target="tpu_custom_call" | custom-call | tf_op jit(solution)/shard_map/pallas_call | solution.py:354
  46.1 0.8 %shard_map.103 = (bf16[128,512]{1,0:T(8,128)(2,1)}, bf16[128,512]{1,0:T(8,128)(2,1)}, bf16[128,512]{1,0:T(8,128)(2,1)}, f32[1,512]{1,0:T(1,128)}) custom-call(bf16[128,512]{1,0:T(8,128)(2,1)S(1)} %get-tuple-element.12.refs_0_, bf16[128,512]{1,0:T(8,128)(2,1)S(1)} %get-tuple-element.13.refs_1_, bf16[128,512]{1,0:T(8,128)(2,1)S(1)} %get-tuple-element.14.refs_2_, ...), custom_call_target="tpu_custom_call" | custom-call | tf_op jit(solution)/shard_map/pallas_call | solution.py:393

commit v3 on v2

--- a/solution.py
+++ b/solution.py
@@ -50,7 +50,7 @@
     z_own, z_all, gr_own, gr_all, gc_own, gc_all,
     att_ref, back_ref, w_ref, dk_acc, dv_acc, qk_ref,
     in_sem, meta_s, meta_r, a2a_s, a2a_r, col_s, col_r, ret_s, ret_r,
-    z_s, z_r, gr_s, gr_r, gc_s, gc_r,
+    z_s, z_r, gr_s, gr_r, gc_s, gc_r, tokens,
 ):
     me = lax.axis_index("seq")
     z = lax.axis_index("head")
@@ -76,15 +76,51 @@
     row_mates = [lax.rem(pos + s, ROW) for s in ORDER]
     col_mates = [lax.rem(row + s, rows) for s in range(1, rows)]
     z_mates = [lax.rem(z + s, zs) for s in sorted(range(1, zs), key=lambda s: -min(s, zs - s))]
+    z_sides = sorted({1 % zs, (zs - 1) % zs} - {0})
+    up, down = row < rows - 1, row > 0
+    y_sides = ((up, row + 1), (down, row - 1))
     barrier = pltpu.get_barrier_semaphore()
     for p in row_mates:
         pl.semaphore_signal(barrier, inc=1, device_id=seq_of(row, p), device_id_type=MESH)
-    for r in col_mates:
-        pl.semaphore_signal(barrier, inc=1, device_id=seq_of(r, pos), device_id_type=MESH)
-    for other in z_mates:
-        pl.semaphore_signal(
-            barrier, inc=1, device_id={"seq": me, "head": other}, device_id_type=MESH
-        )
+    for s in z_sides:
+        other = {"seq": me, "head": lax.rem(z + s, zs)}
+        pl.semaphore_signal(barrier, inc=1, device_id=other, device_id_type=MESH)
+    for near, other in y_sides:
+        @pl.when(near)
+        def _():
+            pl.semaphore_signal(barrier, inc=1, device_id=seq_of(other, pos), device_id_type=MESH)
+
+    y_waves, z_waves = rows - 2, zs // 2 - 1
+
+    def token(wave):
+        if wave < z_waves:
+            for i, s in enumerate(z_sides):
+                pl.semaphore_signal(
+                    tokens.at[1, i, wave], inc=1, device_id_type=MESH,
+                    device_id={"seq": me, "head": lax.rem(z + s, zs)},
+                )
+        if wave < y_waves:
+            for i, (near, other) in enumerate(y_sides):
+                @pl.when(near)
+                def _():
+                    pl.semaphore_signal(
+                        tokens.at[0, i, wave], inc=1, device_id_type=MESH,
+                        device_id=seq_of(other, pos),
+                    )
+
+    def take(wave):
+        if wave < z_waves:
+            for i in range(len(z_sides)):
+                pl.semaphore_wait(tokens.at[1, i, wave], 1)
+        if wave < y_waves:
+            for i, near in enumerate((down, up)):
+                @pl.when(near)
+                def _():
+                    pl.semaphore_wait(tokens.at[0, i, wave], 1)
+
+    def step_tokens(wave):
+        take(wave)
+        token(wave + 1)
 
     def remote(src, dst, ss, rs, target):
         return pltpu.make_async_remote_copy(
@@ -132,7 +168,9 @@
         states[0, 2 * h] = local[:HALF]
         states[0, 2 * h + 1] = local[HALF:]
 
-    pl.semaphore_wait(barrier, len(row_mates) + len(col_mates) + len(z_mates))
+    pl.semaphore_wait(
+        barrier, len(row_mates) + len(z_sides) + up.astype(jnp.int32) + down.astype(jnp.int32)
+    )
 
     def scatter(side):
         for c in range(CHUNKS):
@@ -154,6 +192,20 @@
     for p in row_mates:
         send(meta_own, meta.at[pos], meta_s.at[0], meta_r.at[0], seq_of(row, p))
     scatter(0)
+
+    def before_of(side):
+        return row if side == 0 else rows - 1 - row
+
+    def after_of(side):
+        return rows - 1 - row if side == 0 else row
+
+    token(0)
+    for side in range(2):
+        for step in range(2):
+            @pl.when(before_of(side) <= step)
+            def _():
+                carried[side, step, :HEAD_ROWS] = jnp.full((HEAD_ROWS, DIM), -1.0, F32)
+                carried[side, step, HEAD_ROWS:] = jnp.zeros((HALF, DIM), F32)
 
     def scan_first(side):
         order, seg_of = order_of(side)
@@ -168,30 +220,30 @@
                 totals[side, :HEAD_ROWS] = jnp.broadcast_to(seg_of[-1], (HEAD_ROWS, DIM))
             totals[side, pl.ds(HEAD_ROWS + c * PART, PART)] = run
             for step in (1, 0):
-                move = step + 1 if side == 0 else rows - step - 1
-                send(
-                    totals.at[side, piece(c)], carried.at[side, step, piece(c)],
-                    col_s.at[side], col_r.at[side, step, c],
-                    seq_of(lax.rem(row + move, rows), pos),
-                )
+                @pl.when(after_of(side) > step)
+                def _():
+                    send(
+                        totals.at[side, piece(c)], carried.at[side, step, piece(c)],
+                        col_s.at[side, step], col_r.at[side, step, c],
+                        seq_of(row + (step + 1 if side == 0 else -step - 1), pos),
+                    )
 
     def scan_second(side):
         order, seg_of = order_of(side)
-        before = row if side == 0 else rows - 1 - row
-        near_on = jnp.where(before >= 1, 1.0, 0.0)
         for c in range(CHUNKS):
             for step in range(2):
-                arrived(carried.at[side, step, piece(c)], col_r.at[side, step, c])
+                @pl.when(before_of(side) > step)
+                def _():
+                    arrived(carried.at[side, step, piece(c)], col_r.at[side, step, c])
             if c == 0:
                 near_seg = carried[side, 0, 0:1]
                 far_seg = carried[side, 1, 0:1]
-                near_seg = jnp.where(before >= 1, near_seg, -1.0)
-                far_on = jnp.where(before >= 2, jnp.where(far_seg == near_seg, lam_row, 0.0), 0.0)
+                far_on = jnp.where(far_seg == near_seg, lam_row, 0.0)
                 prev = [near_seg] + seg_of[:-1]
                 factor = [jnp.where(a == b, lam, 0.0) for a, b in zip(seg_of, prev)]
             rows_c = pl.ds(HEAD_ROWS + c * PART, PART)
             part = pl.ds(c * PART, PART)
-            run = carried[side, 0, rows_c] * near_on + far_on * carried[side, 1, rows_c]
+            run = carried[side, 0, rows_c] + far_on * carried[side, 1, rows_c]
             for n in range(ROW):
                 prefixes[side, order[n], part] = run
                 if n < ROW - 1:
@@ -220,13 +272,17 @@
         qk_ref[h, 1] = scores[1]
         att_ref[h] = mm_split_left(scores, v_ref[:, cut], 1, 0)
 
+    step_tokens(0)
     arrived(meta.at[row_others], meta_r.at[0])
     scan_first(0)
+    step_tokens(1)
     prev_row_seg = scan_second(0)
+    step_tokens(2)
     prev_seg = jnp.where(pos == 0, prev_row_seg, meta[lax.rem(pos + ROW - 1, ROW), 0:1, :])
     loads[3].wait()
     loads[6].wait()
     scan_last(0)
+    step_tokens(3)
 
     into_on = seg_col == prev_seg
     squares = jnp.zeros((BLOCK, DIM), F32)
@@ -248,6 +304,7 @@
     z_all[z] = z_own[...]
     if zs > 1:
         arrived(z_all.at[pl.ds(0, zs - 1)], z_r.at[0])
+    step_tokens(4)
     both = z_all[0]
     for i in range(1, zs):
         both = both + z_all[i]
@@ -288,6 +345,7 @@
     inner(0)
     inner(1)
     scan_first(1)
+    step_tokens(5)
     arrived(gr_all.at[row_others], gr_r.at[0])
     total = gr_all[0]
     for a in range(1, ROW):
@@ -320,7 +378,10 @@
     sent(meta.at[row_others], meta_s.at[0])
     for side in range(2):
         sent(states.at[side, row_others], a2a_s.at[side])
-        sent(carried.at[side], col_s.at[side])
+        for step in range(2):
+            @pl.when(after_of(side) > step)
+            def _():
+                sent(carried.at[side, step], col_s.at[side, step])
         sent(prefixes.at[side, row_others], ret_s.at[side])
     if zs > 1:
         sent(z_all.at[pl.ds(0, zs - 1)], z_s.at[0])
@@ -378,11 +439,12 @@
             dma((7,)),
             dma((1,)), dma((1,)),
             dma((2,)), dma((2, CHUNKS)),
-            dma((2,)), dma((2, 2, CHUNKS)),
+            dma((2, 2)), dma((2, 2, CHUNKS)),
             dma((2,)), dma((2,)),
             dma((1,)), dma((1,)),
             dma((1,)), dma((1,)),
             dma((1,)), dma((1,)),
+            pltpu.SemaphoreType.REGULAR((2, 2, 6)),
         ],
         compiler_params=pltpu.CompilerParams(collective_id=0, has_side_effects=True),
     )(

time: 47.1 us -> 44.5 us (0.945)
  the two profiles are of different devices: /device:TPU:1 before, /device:TPU:17 now
where the time goes in v3:
time: 44.5 us; the launch traced here: 44.3 us
  Pallas kernels  43.6 us (98%)
  between operations  0.64 us (1%)
    pallas_call x1, Pallas kernels, local(): pl.pallas_call(functools.partial(kernel, rows, zs, heads), out_shape=(wid...  42.9 us

profile of v3, /device:TPU:17, one launch (start us, length us, event | category | flops | bytes accessed | tf_op | source)
XLA Modules:
  0.0 44.3 jit_solution(2579168828121262295)
XLA Ops:
  0.6 42.9 %shard_map.102 = (bf16[128,512]{1,0:T(8,128)(2,1)S(1)}, bf16[128,512]{1,0:T(8,128)(2,1)S(1)}, bf16[128,512]{1,0:T(8,128)(2,1)S(1)}, f32[1,512]{1,0:T(1,128)S(1)}) custom-call(bf16[128,512]{1,0:T(8,128)(2,1)} %q_hbm.1, bf16[128,512]{1,0:T(8,128)(2,1)} %k_hbm.1, bf16[128,512]{1,0:T(8,128)(2,1)} %v_hbm.1, bf16[128,512]{1,0:T(8,128)(2,1)} %dy_hbm.1, ...), custom_call_target="tpu_custom_call" | custom-call | tf_op jit(solution)/shard_map/pallas_call | solution.py:415
  43.5 0.8 %shard_map.103 = (bf16[128,512]{1,0:T(8,128)(2,1)}, bf16[128,512]{1,0:T(8,128)(2,1)}, bf16[128,512]{1,0:T(8,128)(2,1)}, f32[1,512]{1,0:T(1,128)}) custom-call(bf16[128,512]{1,0:T(8,128)(2,1)S(1)} %get-tuple-element.12.refs_0_, bf16[128,512]{1,0:T(8,128)(2,1)S(1)} %get-tuple-element.13.refs_1_, bf16[128,512]{1,0:T(8,128)(2,1)S(1)} %get-tuple-element.14.refs_2_, ...), custom_call_target="tpu_custom_call" | custom-call | tf_op jit(solution)/shard_map/pallas_call | solution.py:455

commit v4 on v3

--- a/solution.py
+++ b/solution.py
@@ -10,9 +10,9 @@
 DIM = 128
 ROW = 8
 BLOCK = 128
-HALF = 64
+CHIPS = ROW // 2
 CHUNKS = 4
-PART = HALF // CHUNKS
+PART = DIM // CHUNKS
 HEAD_ROWS = 8
 MESH = pl.DeviceIdType.MESH
 F32 = jnp.float32
@@ -50,12 +50,13 @@
     z_own, z_all, gr_own, gr_all, gc_own, gc_all,
     att_ref, back_ref, w_ref, dk_acc, dv_acc, qk_ref,
     in_sem, meta_s, meta_r, a2a_s, a2a_r, col_s, col_r, ret_s, ret_r,
-    z_s, z_r, gr_s, gr_r, gc_s, gc_r, tokens,
+    z_s, z_r, gr_s, gr_r, gc_s, gc_r, tokens, edge, edge_s, edge_r,
 ):
     me = lax.axis_index("seq")
     z = lax.axis_index("head")
     row = me // ROW
     pos = lax.rem(me, ROW)
+    chip, core = pos // 2, lax.rem(pos, 2)
     features = float(zs * heads * DIM)
 
     loads = [
@@ -153,7 +154,7 @@
     meta[pos] = meta_own[...]
 
     inverse = [1.0 / jnp.full((1, DIM), span_ref[h], F32) for h in range(heads)]
-    own_inverse = 1.0 / jnp.full((1, DIM), span_ref[pos // 2], F32)
+    own_inverse = 1.0 / jnp.full((1, DIM), span_ref[chip], F32)
     lam = jnp.exp(-float(BLOCK) * own_inverse)
     lam_row = jnp.exp(-float(BLOCK * ROW) * own_inverse)
 
@@ -165,8 +166,7 @@
         local = mm_split_right(
             k_ref[:, cut], split(v_ref[:, cut].astype(F32) * tail), 0, 0
         )
-        states[0, 2 * h] = local[:HALF]
-        states[0, 2 * h + 1] = local[HALF:]
+        states[0, h] = local
 
     pl.semaphore_wait(
         barrier, len(row_mates) + len(z_sides) + up.astype(jnp.int32) + down.astype(jnp.int32)
@@ -175,12 +175,23 @@
     def scatter(side):
         for c in range(CHUNKS):
             part = pl.ds(c * PART, PART)
-            for p in row_mates:
+            for d in (2, 1, 3):
+                h = lax.rem(chip + d, CHIPS)
                 send(
-                    states.at[side, p, part], gathered.at[side, pos, part],
-                    a2a_s.at[side], a2a_r.at[side, c], seq_of(row, p),
+                    states.at[side, h, part], gathered.at[side, pos, part],
+                    a2a_s.at[side], a2a_r.at[side, c], seq_of(row, 2 * h + 1),
                 )
-        gathered[side, pos] = states[side, pos]
+
+            @pl.when(core == 0)
+            def _():
+                send(
+                    states.at[side, chip, part], gathered.at[side, pos, part],
+                    a2a_s.at[side], a2a_r.at[side, c], seq_of(row, pos + 1),
+                )
+
+        @pl.when(core == 1)
+        def _():
+            gathered[side, pos] = states[side, chip]
 
     def piece(c):
         return pl.ds(HEAD_ROWS + c * PART, PART) if c else pl.ds(0, HEAD_ROWS + PART)
@@ -205,7 +216,7 @@
             @pl.when(before_of(side) <= step)
             def _():
                 carried[side, step, :HEAD_ROWS] = jnp.full((HEAD_ROWS, DIM), -1.0, F32)
-                carried[side, step, HEAD_ROWS:] = jnp.zeros((HALF, DIM), F32)
+                carried[side, step, HEAD_ROWS:] = jnp.zeros((DIM, DIM), F32)
 
     def scan_first(side):
         order, seg_of = order_of(side)
@@ -236,6 +247,11 @@
                 def _():
                     arrived(carried.at[side, step, piece(c)], col_r.at[side, step, c])
             if c == 0:
+                if side == 0:
+                    @pl.when(pos == 1)
+                    def _():
+                        send(carried.at[0, 0, pl.ds(0, HEAD_ROWS)], edge,
+                             edge_s.at[0], edge_r.at[0], seq_of(row, pos - 1))
                 near_seg = carried[side, 0, 0:1]
                 far_seg = carried[side, 1, 0:1]
                 far_on = jnp.where(far_seg == near_seg, lam_row, 0.0)
@@ -250,14 +266,19 @@
                     run = gathered[side, order[n], part] + factor[n] * run
             for p in row_mates:
                 send(
-                    prefixes.at[side, p, part], state_in.at[side, pos, part],
+                    prefixes.at[side, p, part], state_in.at[side, chip, part],
                     ret_s.at[side], ret_r.at[side], seq_of(row, p),
                 )
-        state_in[side, pos] = prefixes[side, pos]
-        return near_seg
+        state_in[side, chip] = prefixes[side, pos]
 
     def scan_last(side):
-        arrived(state_in.at[side, row_others], ret_r.at[side])
+        @pl.when(core == 0)
+        def _():
+            arrived(state_in.at[side], ret_r.at[side])
+
+        @pl.when(core == 1)
+        def _():
+            arrived(state_in.at[side, pl.ds(0, CHIPS - 1)], ret_r.at[side])
 
     loads[2].wait()
     causal = t_col >= s_row
@@ -274,15 +295,20 @@
 
     step_tokens(0)
     arrived(meta.at[row_others], meta_r.at[0])
-    scan_first(0)
+    pl.when(core == 1)(lambda: scan_first(0))
     step_tokens(1)
-    prev_row_seg = scan_second(0)
+    pl.when(core == 1)(lambda: scan_second(0))
     step_tokens(2)
-    prev_seg = jnp.where(pos == 0, prev_row_seg, meta[lax.rem(pos + ROW - 1, ROW), 0:1, :])
     loads[3].wait()
     loads[6].wait()
     scan_last(0)
     step_tokens(3)
+
+    @pl.when(pos == 0)
+    def _():
+        arrived(edge, edge_r.at[0])
+
+    prev_seg = jnp.where(pos == 0, edge[0:1], meta[lax.rem(pos + ROW - 1, ROW), 0:1, :])
 
     into_on = seg_col == prev_seg
     squares = jnp.zeros((BLOCK, DIM), F32)
@@ -290,7 +316,7 @@
     for h in range(heads):
         cut = slice(h * DIM, (h + 1) * DIM)
         into = jnp.where(into_on, jnp.exp(-(t_col + 1.0) * inverse[h]), 0.0)
-        state = split(state_in[0, 2 * h:2 * h + 2].reshape(DIM, DIM))
+        state = split(state_in[0, h])
         att = att_ref[h] + into * mm_split_right(q_ref[:, cut], state, 1, 0)
         att_ref[h] = att
         squares = squares + att * att
@@ -323,8 +349,7 @@
         gr_own[h:h + 1] = jnp.sum(scaled * att, axis=0, keepdims=True)
         start = jnp.where(seg_col == first_own, jnp.exp(-t_col * inverse[h]), 0.0)
         local = mm_split_right(q_ref[:, cut], split(back * start), 0, 0)
-        states[1, 2 * h] = local[:HALF]
-        states[1, 2 * h + 1] = local[HALF:]
+        states[1, h] = local
     scatter(1)
     for p in row_mates:
         send(gr_own, gr_all.at[pos], gr_s.at[0], gr_r.at[0], seq_of(row, p))
@@ -336,7 +361,7 @@
         weights = w_ref[h]
         grads = split(mm_split_left(back, v_ref[:, cut], 1, 1) * weights)
         into = jnp.where(into_on, jnp.exp(-(t_col + 1.0) * inverse[h]), 0.0)
-        state = split(state_in[0, 2 * h:2 * h + 2].reshape(DIM, DIM))
+        state = split(state_in[0, h])
         dq = mm_split_left(grads, k_ref[:, cut], 1, 0) + into * mm_split_both(back, state, 1, 1)
         dq_ref[:, cut] = dq.astype(BF16)
         dk_acc[h] = mm_split_left(grads, q_ref[:, cut], 0, 0)
@@ -344,7 +369,7 @@
 
     inner(0)
     inner(1)
-    scan_first(1)
+    pl.when(core == 1)(lambda: scan_first(1))
     step_tokens(5)
     arrived(gr_all.at[row_others], gr_r.at[0])
     total = gr_all[0]
@@ -355,8 +380,10 @@
     for r in col_mates:
         send(gc_own, gc_all.at[row], gc_s.at[0], gc_r.at[0], seq_of(r, pos))
     inner(2)
-    next_row_seg = scan_second(1)
-    next_seg = jnp.where(pos == ROW - 1, next_row_seg, meta[lax.rem(pos + 1, ROW), 1:2, :])
+    pl.when(core == 1)(lambda: scan_second(1))
+    next_seg = jnp.where(
+        pos == ROW - 1, carried[1, 0, 0:1], meta[lax.rem(pos + 1, ROW), 1:2, :]
+    )
     inner(3)
     arrived(gc_all.at[pl.ds(0, rows - 1)], gc_r.at[0])
     total = gc_all[0]
@@ -370,19 +397,30 @@
     for h in range(heads):
         cut = slice(h * DIM, (h + 1) * DIM)
         weight = jnp.where(next_on, jnp.exp((t_col - float(BLOCK)) * inverse[h]), 0.0)
-        grad = split(state_in[1, 2 * h:2 * h + 2].reshape(DIM, DIM))
+        grad = split(state_in[1, h])
         dk = dk_acc[h] + weight * mm_split_right(v_ref[:, cut], grad, 1, 1)
         dv = dv_acc[h] + weight * mm_split_right(k_ref[:, cut], grad, 1, 0)
         dk_ref[:, cut] = dk.astype(BF16)
         dv_ref[:, cut] = dv.astype(BF16)
     sent(meta.at[row_others], meta_s.at[0])
     for side in range(2):
-        sent(states.at[side, row_others], a2a_s.at[side])
-        for step in range(2):
-            @pl.when(after_of(side) > step)
-            def _():
-                sent(carried.at[side, step], col_s.at[side, step])
-        sent(prefixes.at[side, row_others], ret_s.at[side])
+        @pl.when(core == 0)
+        def _():
+            sent(states.at[side], a2a_s.at[side])
+
+        @pl.when(core == 1)
+        def _():
+            sent(states.at[side, pl.ds(0, CHIPS - 1)], a2a_s.at[side])
+            sent(prefixes.at[side, row_others], ret_s.at[side])
+            for step in range(2):
+                @pl.when(after_of(side) > step)
+                def _():
+                    sent(carried.at[side, step], col_s.at[side, step])
+
+    @pl.when(pos == 1)
+    def _():
+        sent(edge, edge_s.at[0])
+
     if zs > 1:
         sent(z_all.at[pl.ds(0, zs - 1)], z_s.at[0])
     sent(gr_all.at[row_others], gr_s.at[0])
@@ -409,7 +447,8 @@
     near = pl.BlockSpec(memory_space=pltpu.VMEM)
     wide = pltpu.VMEM((BLOCK, width), BF16)
     square = pltpu.VMEM((heads, DIM, DIM), F32)
-    pieces = pltpu.VMEM((2, ROW, HALF, DIM), F32)
+    pieces = pltpu.VMEM((2, ROW, DIM, DIM), F32)
+    per_head = pltpu.VMEM((2, heads, DIM, DIM), F32)
     dma = pltpu.SemaphoreType.DMA
     kept = pltpu.VMEM((1, width), F32)
     results = pl.pallas_call(
@@ -422,12 +461,12 @@
             pltpu.VMEM((1, BLOCK), jnp.int32), pltpu.SMEM((heads,), F32), kept,
             pltpu.VMEM((8, DIM), F32),
             pltpu.VMEM((ROW, 8, DIM), F32),
+            per_head,
             pieces,
+            pltpu.VMEM((2, HEAD_ROWS + DIM, DIM), F32),
+            pltpu.VMEM((2, 2, HEAD_ROWS + DIM, DIM), F32),
             pieces,
-            pltpu.VMEM((2, HEAD_ROWS + HALF, DIM), F32),
-            pltpu.VMEM((2, 2, HEAD_ROWS + HALF, DIM), F32),
-            pieces,
-            pieces,
+            per_head,
             pltpu.VMEM((2, DIM), F32),
             pltpu.VMEM((zs, 2, DIM), F32),
             pltpu.VMEM((heads, DIM), F32),
@@ -445,6 +484,7 @@
             dma((1,)), dma((1,)),
             dma((1,)), dma((1,)),
             pltpu.SemaphoreType.REGULAR((2, 2, 6)),
+            pltpu.VMEM((HEAD_ROWS, DIM), F32), dma((1,)), dma((1,)),
         ],
         compiler_params=pltpu.CompilerParams(collective_id=0, has_side_effects=True),
     )(

time: 44.5 us -> 43.1 us (0.969)
  Pallas kernels: 43.6 us -> 42.3 us
    pallas_call x1, Pallas kernels: 42.9 us -> 41.5 us  [local(): pl.pallas_call(functools.partial(kernel, rows, zs, heads), out_shape=(wid...]
where the time goes in v4:
time: 43.1 us; the launch traced here: 43 us
  Pallas kernels  42.3 us (98%)
  between operations  0.64 us (1%)
    pallas_call x1, Pallas kernels, local(): pl.pallas_call(functools.partial(kernel, rows, zs, heads), out_shape=(wid...  41.5 us

profile of v4, /device:TPU:17, one launch (start us, length us, event | category | flops | bytes accessed | tf_op | source)
XLA Modules:
  0.0 43.0 jit_solution(13234481397531615405)
XLA Ops:
  0.6 41.5 %shard_map.102 = (bf16[128,512]{1,0:T(8,128)(2,1)S(1)}, bf16[128,512]{1,0:T(8,128)(2,1)S(1)}, bf16[128,512]{1,0:T(8,128)(2,1)S(1)}, f32[1,512]{1,0:T(1,128)S(1)}) custom-call(bf16[128,512]{1,0:T(8,128)(2,1)} %q_hbm.1, bf16[128,512]{1,0:T(8,128)(2,1)} %k_hbm.1, bf16[128,512]{1,0:T(8,128)(2,1)} %v_hbm.1, bf16[128,512]{1,0:T(8,128)(2,1)} %dy_hbm.1, ...), custom_call_target="tpu_custom_call" | custom-call | tf_op jit(solution)/shard_map/pallas_call | solution.py:454
  42.2 0.8 %shard_map.103 = (bf16[128,512]{1,0:T(8,128)(2,1)}, bf16[128,512]{1,0:T(8,128)(2,1)}, bf16[128,512]{1,0:T(8,128)(2,1)}, f32[1,512]{1,0:T(1,128)}) custom-call(bf16[128,512]{1,0:T(8,128)(2,1)S(1)} %get-tuple-element.12.refs_0_, bf16[128,512]{1,0:T(8,128)(2,1)S(1)} %get-tuple-element.13.refs_1_, bf16[128,512]{1,0:T(8,128)(2,1)S(1)} %get-tuple-element.14.refs_2_, ...), custom_call_target="tpu_custom_call" | custom-call | tf_op jit(solution)/shard_map/pallas_call | solution.py:495

commit v5 on v4

--- a/solution.py
+++ b/solution.py
@@ -11,7 +11,7 @@
 ROW = 8
 BLOCK = 128
 CHIPS = ROW // 2
-CHUNKS = 4
+CHUNKS = 8
 PART = DIM // CHUNKS
 HEAD_ROWS = 8
 MESH = pl.DeviceIdType.MESH
@@ -51,6 +51,7 @@
     att_ref, back_ref, w_ref, dk_acc, dv_acc, qk_ref,
     in_sem, meta_s, meta_r, a2a_s, a2a_r, col_s, col_r, ret_s, ret_r,
     z_s, z_r, gr_s, gr_r, gc_s, gc_r, tokens, edge, edge_s, edge_r,
+    into_ref, next_ref, start_ref, gdy_ref, start_gdy, start_att, q_turned,
 ):
     me = lax.axis_index("seq")
     z = lax.axis_index("head")
@@ -97,7 +98,7 @@
         if wave < z_waves:
             for i, s in enumerate(z_sides):
                 pl.semaphore_signal(
-                    tokens.at[1, i, wave], inc=1, device_id_type=MESH,
+                    tokens.at[1, i], inc=1, device_id_type=MESH,
                     device_id={"seq": me, "head": lax.rem(z + s, zs)},
                 )
         if wave < y_waves:
@@ -105,19 +106,19 @@
                 @pl.when(near)
                 def _():
                     pl.semaphore_signal(
-                        tokens.at[0, i, wave], inc=1, device_id_type=MESH,
+                        tokens.at[0, i], inc=1, device_id_type=MESH,
                         device_id=seq_of(other, pos),
                     )
 
     def take(wave):
         if wave < z_waves:
             for i in range(len(z_sides)):
-                pl.semaphore_wait(tokens.at[1, i, wave], 1)
+                pl.semaphore_wait(tokens.at[1, i], 1)
         if wave < y_waves:
             for i, near in enumerate((down, up)):
                 @pl.when(near)
                 def _():
-                    pl.semaphore_wait(tokens.at[0, i, wave], 1)
+                    pl.semaphore_wait(tokens.at[0, i], 1)
 
     def step_tokens(wave):
         take(wave)
@@ -149,8 +150,8 @@
     seg_col = seg_tile.T
     first_own = jnp.broadcast_to(seg_row[:, 0:1], (1, DIM))
     last_own = jnp.broadcast_to(seg_row[:, BLOCK - 1:BLOCK], (1, DIM))
-    tile_row = lax.broadcasted_iota(jnp.int32, (8, DIM), 0)
-    meta_own[...] = jnp.where(tile_row == 0, last_own, first_own)
+    meta_own[0:1] = last_own
+    meta_own[1:2] = first_own
     meta[pos] = meta_own[...]
 
     inverse = [1.0 / jnp.full((1, DIM), span_ref[h], F32) for h in range(heads)]
@@ -158,13 +159,16 @@
     lam = jnp.exp(-float(BLOCK) * own_inverse)
     lam_row = jnp.exp(-float(BLOCK * ROW) * own_inverse)
 
+    for h in range(heads):
+        att_ref[h] = jnp.where(
+            seg_col == last_own, jnp.exp((t_col - (BLOCK - 1.0)) * inverse[h]), 0.0
+        )
     loads[0].wait()
     loads[1].wait()
     for h in range(heads):
         cut = slice(h * DIM, (h + 1) * DIM)
-        tail = jnp.where(seg_col == last_own, jnp.exp((t_col - (BLOCK - 1.0)) * inverse[h]), 0.0)
         local = mm_split_right(
-            k_ref[:, cut], split(v_ref[:, cut].astype(F32) * tail), 0, 0
+            k_ref[:, cut], split(v_ref[:, cut].astype(F32) * att_ref[h]), 0, 0
         )
         states[0, h] = local
 
@@ -179,14 +183,14 @@
                 h = lax.rem(chip + d, CHIPS)
                 send(
                     states.at[side, h, part], gathered.at[side, pos, part],
-                    a2a_s.at[side], a2a_r.at[side, c], seq_of(row, 2 * h + 1),
+                    a2a_s.at[0], a2a_r.at[c], seq_of(row, 2 * h + 1),
                 )
 
             @pl.when(core == 0)
             def _():
                 send(
                     states.at[side, chip, part], gathered.at[side, pos, part],
-                    a2a_s.at[side], a2a_r.at[side, c], seq_of(row, pos + 1),
+                    a2a_s.at[0], a2a_r.at[c], seq_of(row, pos + 1),
                 )
 
         @pl.when(core == 1)
@@ -215,15 +219,15 @@
         for step in range(2):
             @pl.when(before_of(side) <= step)
             def _():
-                carried[side, step, :HEAD_ROWS] = jnp.full((HEAD_ROWS, DIM), -1.0, F32)
-                carried[side, step, HEAD_ROWS:] = jnp.zeros((DIM, DIM), F32)
+                carried[2 * side + step, :HEAD_ROWS] = jnp.full((HEAD_ROWS, DIM), -1.0, F32)
+                carried[2 * side + step, HEAD_ROWS:] = jnp.zeros((DIM, DIM), F32)
 
     def scan_first(side):
         order, seg_of = order_of(side)
         factor = [jnp.where(seg_of[n] == seg_of[n - 1], lam, 0.0) for n in range(1, ROW)]
         for c in range(CHUNKS):
             part = pl.ds(c * PART, PART)
-            arrived(gathered.at[side, row_others, part], a2a_r.at[side, c])
+            arrived(gathered.at[side, row_others, part], a2a_r.at[c])
             run = gathered[side, order[0], part]
             for n in range(1, ROW):
                 run = gathered[side, order[n], part] + factor[n - 1] * run
@@ -234,32 +238,36 @@
                 @pl.when(after_of(side) > step)
                 def _():
                     send(
-                        totals.at[side, piece(c)], carried.at[side, step, piece(c)],
-                        col_s.at[side, step], col_r.at[side, step, c],
+                        totals.at[side, piece(c)], carried.at[2 * side + step, piece(c)],
+                        col_s.at[0], col_r.at[side, c],
                         seq_of(row + (step + 1 if side == 0 else -step - 1), pos),
                     )
 
     def scan_second(side):
         order, seg_of = order_of(side)
         for c in range(CHUNKS):
-            for step in range(2):
-                @pl.when(before_of(side) > step)
-                def _():
-                    arrived(carried.at[side, step, piece(c)], col_r.at[side, step, c])
+            @pl.when(before_of(side) == 1)
+            def _():
+                arrived(carried.at[2 * side, piece(c)], col_r.at[side, c])
+
+            @pl.when(before_of(side) > 1)
+            def _():
+                arrived(carried.at[pl.ds(2 * side, 2), piece(c)], col_r.at[side, c])
+
             if c == 0:
                 if side == 0:
                     @pl.when(pos == 1)
                     def _():
-                        send(carried.at[0, 0, pl.ds(0, HEAD_ROWS)], edge,
+                        send(carried.at[0, pl.ds(0, HEAD_ROWS)], edge,
                              edge_s.at[0], edge_r.at[0], seq_of(row, pos - 1))
-                near_seg = carried[side, 0, 0:1]
-                far_seg = carried[side, 1, 0:1]
+                near_seg = carried[2 * side, 0:1]
+                far_seg = carried[2 * side + 1, 0:1]
                 far_on = jnp.where(far_seg == near_seg, lam_row, 0.0)
                 prev = [near_seg] + seg_of[:-1]
                 factor = [jnp.where(a == b, lam, 0.0) for a, b in zip(seg_of, prev)]
             rows_c = pl.ds(HEAD_ROWS + c * PART, PART)
             part = pl.ds(c * PART, PART)
-            run = carried[side, 0, rows_c] + far_on * carried[side, 1, rows_c]
+            run = carried[2 * side, rows_c] + far_on * carried[2 * side + 1, rows_c]
             for n in range(ROW):
                 prefixes[side, order[n], part] = run
                 if n < ROW - 1:
@@ -267,18 +275,20 @@
             for p in row_mates:
                 send(
                     prefixes.at[side, p, part], state_in.at[side, chip, part],
-                    ret_s.at[side], ret_r.at[side], seq_of(row, p),
+                    ret_s.at[0], ret_r.at[lax.rem(chip + CHIPS - p // 2, CHIPS)],
+                    seq_of(row, p),
                 )
         state_in[side, chip] = prefixes[side, pos]
 
-    def scan_last(side):
-        @pl.when(core == 0)
-        def _():
-            arrived(state_in.at[side], ret_r.at[side])
-
-        @pl.when(core == 1)
-        def _():
-            arrived(state_in.at[side, pl.ds(0, CHIPS - 1)], ret_r.at[side])
+    def next_head(side, d):
+        head = lax.rem(chip + d, CHIPS)
+        if d:
+            arrived(state_in.at[side, head], ret_r.at[d])
+        else:
+            @pl.when(core == 0)
+            def _():
+                arrived(state_in.at[side, head], ret_r.at[d])
+        return head, pl.ds(pl.multiple_of(head * DIM, DIM), DIM)
 
     loads[2].wait()
     causal = t_col >= s_row
@@ -292,16 +302,21 @@
         qk_ref[h, 0] = scores[0]
         qk_ref[h, 1] = scores[1]
         att_ref[h] = mm_split_left(scores, v_ref[:, cut], 1, 0)
-
+        into_ref[h] = jnp.exp(-(t_col + 1.0) * inverse[h])
+        next_ref[h] = jnp.exp((t_col - float(BLOCK)) * inverse[h])
+        start_ref[h] = jnp.where(seg_col == first_own, jnp.exp(-t_col * inverse[h]), 0.0)
+
+    loads[3].wait()
+    loads[6].wait()
+    for h in range(heads):
+        cut = slice(h * DIM, (h + 1) * DIM)
+        gdy_ref[h] = gain_ref[:, cut] * dy_ref[:, cut].astype(F32)
     step_tokens(0)
     arrived(meta.at[row_others], meta_r.at[0])
     pl.when(core == 1)(lambda: scan_first(0))
     step_tokens(1)
     pl.when(core == 1)(lambda: scan_second(0))
     step_tokens(2)
-    loads[3].wait()
-    loads[6].wait()
-    scan_last(0)
     step_tokens(3)
 
     @pl.when(pos == 0)
@@ -309,18 +324,18 @@
         arrived(edge, edge_r.at[0])
 
     prev_seg = jnp.where(pos == 0, edge[0:1], meta[lax.rem(pos + ROW - 1, ROW), 0:1, :])
-
     into_on = seg_col == prev_seg
+    for h in range(heads):
+        into_ref[h] = jnp.where(into_on, into_ref[h], 0.0)
     squares = jnp.zeros((BLOCK, DIM), F32)
     crosses = jnp.zeros((BLOCK, DIM), F32)
-    for h in range(heads):
-        cut = slice(h * DIM, (h + 1) * DIM)
-        into = jnp.where(into_on, jnp.exp(-(t_col + 1.0) * inverse[h]), 0.0)
+    for d in (0, 1, 3, 2):
+        h, cut = next_head(0, d)
         state = split(state_in[0, h])
-        att = att_ref[h] + into * mm_split_right(q_ref[:, cut], state, 1, 0)
+        att = att_ref[h] + into_ref[h] * mm_split_right(q_ref[:, cut], state, 1, 0)
         att_ref[h] = att
         squares = squares + att * att
-        crosses = crosses + dy_ref[:, cut].astype(F32) * gain_ref[:, cut] * att
+        crosses = crosses + gdy_ref[h] * att
     square_row = jnp.sum(squares.T, axis=0, keepdims=True)
     cross_row = jnp.sum(crosses.T, axis=0, keepdims=True)
     z_own[0:1] = square_row
@@ -328,6 +343,10 @@
     for other in z_mates:
         send(z_own, z_all.at[z], z_s.at[0], z_r.at[0], {"seq": me, "head": other})
     z_all[z] = z_own[...]
+    for h in range(heads):
+        start_gdy[h] = start_ref[h] * gdy_ref[h]
+        start_att[h] = start_ref[h] * att_ref[h]
+        q_turned[h] = q_ref[:, h * DIM:(h + 1) * DIM].T
     if zs > 1:
         arrived(z_all.at[pl.ds(0, zs - 1)], z_r.at[0])
     step_tokens(4)
@@ -340,17 +359,14 @@
     off = jnp.broadcast_to(off_row, (BLOCK, DIM)).T
 
     for h in range(heads):
+        scaled = split(inv * start_gdy[h] - off * start_att[h])
+        states[1, h] = mm_split_right(q_turned[h], scaled, 1, 0)
+    scatter(1)
+    for h in range(heads):
         cut = slice(h * DIM, (h + 1) * DIM)
-        dy = dy_ref[:, cut].astype(F32)
         att = att_ref[h]
-        scaled = dy * inv
-        back = gain_ref[:, cut] * scaled - att * off
-        back_ref[h] = back
-        gr_own[h:h + 1] = jnp.sum(scaled * att, axis=0, keepdims=True)
-        start = jnp.where(seg_col == first_own, jnp.exp(-t_col * inverse[h]), 0.0)
-        local = mm_split_right(q_ref[:, cut], split(back * start), 0, 0)
-        states[1, h] = local
-    scatter(1)
+        back_ref[h] = gdy_ref[h] * inv - att * off
+        gr_own[h:h + 1] = jnp.sum(dy_ref[:, cut].astype(F32) * inv * att, axis=0, keepdims=True)
     for p in row_mates:
         send(gr_own, gr_all.at[pos], gr_s.at[0], gr_r.at[0], seq_of(row, p))
     gr_all[pos] = gr_own[...]
@@ -360,7 +376,7 @@
         back = split(back_ref[h])
         weights = w_ref[h]
         grads = split(mm_split_left(back, v_ref[:, cut], 1, 1) * weights)
-        into = jnp.where(into_on, jnp.exp(-(t_col + 1.0) * inverse[h]), 0.0)
+        into = into_ref[h]
         state = split(state_in[0, h])
         dq = mm_split_left(grads, k_ref[:, cut], 1, 0) + into * mm_split_both(back, state, 1, 1)
         dq_ref[:, cut] = dq.astype(BF16)
@@ -382,7 +398,7 @@
     inner(2)
     pl.when(core == 1)(lambda: scan_second(1))
     next_seg = jnp.where(
-        pos == ROW - 1, carried[1, 0, 0:1], meta[lax.rem(pos + 1, ROW), 1:2, :]
+        pos == ROW - 1, carried[2, 0:1], meta[lax.rem(pos + 1, ROW), 1:2, :]
     )
     inner(3)
     arrived(gc_all.at[pl.ds(0, rows - 1)], gc_r.at[0])
@@ -391,31 +407,31 @@
         total = total + gc_all[a]
     for h in range(heads):
         gg_ref[:, h * DIM:(h + 1) * DIM] = total[h:h + 1]
-    scan_last(1)
-
     next_on = seg_col == next_seg
     for h in range(heads):
-        cut = slice(h * DIM, (h + 1) * DIM)
-        weight = jnp.where(next_on, jnp.exp((t_col - float(BLOCK)) * inverse[h]), 0.0)
+        next_ref[h] = jnp.where(next_on, next_ref[h], 0.0)
+    for d in (0, 1, 3, 2):
+        h, cut = next_head(1, d)
+        weight = next_ref[h]
         grad = split(state_in[1, h])
         dk = dk_acc[h] + weight * mm_split_right(v_ref[:, cut], grad, 1, 1)
         dv = dv_acc[h] + weight * mm_split_right(k_ref[:, cut], grad, 1, 0)
         dk_ref[:, cut] = dk.astype(BF16)
         dv_ref[:, cut] = dv.astype(BF16)
     sent(meta.at[row_others], meta_s.at[0])
-    for side in range(2):
-        @pl.when(core == 0)
-        def _():
-            sent(states.at[side], a2a_s.at[side])
-
-        @pl.when(core == 1)
-        def _():
-            sent(states.at[side, pl.ds(0, CHIPS - 1)], a2a_s.at[side])
-            sent(prefixes.at[side, row_others], ret_s.at[side])
-            for step in range(2):
-                @pl.when(after_of(side) > step)
-                def _():
-                    sent(carried.at[side, step], col_s.at[side, step])
+    @pl.when(core == 0)
+    def _():
+        sent(states, a2a_s.at[0])
+
+    @pl.when(core == 1)
+    def _():
+        sent(states.at[:, pl.ds(0, CHIPS - 1)], a2a_s.at[0])
+        sent(prefixes.at[:, row_others], ret_s.at[0])
+        moved = jnp.minimum(row, 2) + jnp.minimum(rows - 1 - row, 2)
+        for n in (2, 3, 4):
+            @pl.when(moved == n)
+            def _():
+                sent(carried.at[pl.ds(0, n)], col_s.at[0])
 
     @pl.when(pos == 1)
     def _():
@@ -459,12 +475,12 @@
         scratch_shapes=[
             wide, wide, wide, wide,
             pltpu.VMEM((1, BLOCK), jnp.int32), pltpu.SMEM((heads,), F32), kept,
-            pltpu.VMEM((8, DIM), F32),
-            pltpu.VMEM((ROW, 8, DIM), F32),
+            pltpu.VMEM((2, DIM), F32),
+            pltpu.VMEM((ROW, 2, DIM), F32),
             per_head,
             pieces,
             pltpu.VMEM((2, HEAD_ROWS + DIM, DIM), F32),
-            pltpu.VMEM((2, 2, HEAD_ROWS + DIM, DIM), F32),
+            pltpu.VMEM((4, HEAD_ROWS + DIM, DIM), F32),
             pieces,
             per_head,
             pltpu.VMEM((2, DIM), F32),
@@ -477,14 +493,16 @@
             pltpu.VMEM((heads, 2, DIM, DIM), BF16),
             dma((7,)),
             dma((1,)), dma((1,)),
-            dma((2,)), dma((2, CHUNKS)),
-            dma((2, 2)), dma((2, 2, CHUNKS)),
-            dma((2,)), dma((2,)),
+            dma((1,)), dma((CHUNKS,)),
+            dma((1,)), dma((2, CHUNKS)),
+            dma((1,)), dma((CHIPS,)),
             dma((1,)), dma((1,)),
             dma((1,)), dma((1,)),
             dma((1,)), dma((1,)),
-            pltpu.SemaphoreType.REGULAR((2, 2, 6)),
+            pltpu.SemaphoreType.REGULAR((2, 2)),
             pltpu.VMEM((HEAD_ROWS, DIM), F32), dma((1,)), dma((1,)),
+            square, square, square, square, square, square,
+            pltpu.VMEM((heads, DIM, DIM), BF16),
         ],
         compiler_params=pltpu.CompilerParams(collective_id=0, has_side_effects=True),
     )(

time: 43.1 us -> 42.2 us (0.979)
  Pallas kernels: 42.3 us -> 41.4 us
    pallas_call x1, Pallas kernels: 41.5 us -> 40.6 us  [local(): pl.pallas_call(functools.partial(kernel, rows, zs, heads), out_shape=(wid...]
where the time goes in v5:
time: 42.2 us; the launch traced here: 42 us
  Pallas kernels  41.4 us (98%)
  between operations  0.64 us (2%)
    pallas_call x1, Pallas kernels, local(): pl.pallas_call(functools.partial(kernel, rows, zs, heads), out_shape=(wid...  40.6 us

profile of v5, /device:TPU:17, one launch (start us, length us, event | category | flops | bytes accessed | tf_op | source)
XLA Modules:
  0.0 42.0 jit_solution(14182413064066309435)
XLA Ops:
  0.6 40.6 %shard_map.102 = (bf16[128,512]{1,0:T(8,128)(2,1)S(1)}, bf16[128,512]{1,0:T(8,128)(2,1)S(1)}, bf16[128,512]{1,0:T(8,128)(2,1)S(1)}, f32[1,512]{1,0:T(1,128)S(1)}) custom-call(bf16[128,512]{1,0:T(8,128)(2,1)} %q_hbm.1, bf16[128,512]{1,0:T(8,128)(2,1)} %k_hbm.1, bf16[128,512]{1,0:T(8,128)(2,1)} %v_hbm.1, bf16[128,512]{1,0:T(8,128)(2,1)} %dy_hbm.1, ...), custom_call_target="tpu_custom_call" | custom-call | tf_op jit(solution)/shard_map/pallas_call | solution.py:470
  41.3 0.8 %shard_map.103 = (bf16[128,512]{1,0:T(8,128)(2,1)}, bf16[128,512]{1,0:T(8,128)(2,1)}, bf16[128,512]{1,0:T(8,128)(2,1)}, f32[1,512]{1,0:T(1,128)}) custom-call(bf16[128,512]{1,0:T(8,128)(2,1)S(1)} %get-tuple-element.12.refs_0_, bf16[128,512]{1,0:T(8,128)(2,1)S(1)} %get-tuple-element.13.refs_1_, bf16[128,512]{1,0:T(8,128)(2,1)S(1)} %get-tuple-element.14.refs_2_, ...), custom_call_target="tpu_custom_call" | custom-call | tf_op jit(solution)/shard_map/pallas_call | solution.py:513

commit v6 on v5

--- a/solution.py
+++ b/solution.py
@@ -52,6 +52,7 @@
     in_sem, meta_s, meta_r, a2a_s, a2a_r, col_s, col_r, ret_s, ret_r,
     z_s, z_r, gr_s, gr_r, gc_s, gc_r, tokens, edge, edge_s, edge_r,
     into_ref, next_ref, start_ref, gdy_ref, start_gdy, start_att, q_turned,
+    pair, landed, lam_ref, pair_s, pair_r, pass_s,
 ):
     me = lax.axis_index("seq")
     z = lax.axis_index("head")
@@ -157,6 +158,8 @@
     inverse = [1.0 / jnp.full((1, DIM), span_ref[h], F32) for h in range(heads)]
     own_inverse = 1.0 / jnp.full((1, DIM), span_ref[chip], F32)
     lam = jnp.exp(-float(BLOCK) * own_inverse)
+    for h in range(heads):
+        lam_ref[h:h + 1] = jnp.exp(-float(BLOCK) * inverse[h])
     lam_row = jnp.exp(-float(BLOCK * ROW) * own_inverse)
 
     for h in range(heads):
@@ -192,6 +195,11 @@
                     states.at[side, chip, part], gathered.at[side, pos, part],
                     a2a_s.at[0], a2a_r.at[c], seq_of(row, pos + 1),
                 )
+
+        if side == 0:
+            @pl.when(core == 0)
+            def _():
+                send(states.at[0], pair, pair_s.at[0], pair_r.at[0], seq_of(row, pos + 1))
 
         @pl.when(core == 1)
         def _():
@@ -269,25 +277,50 @@
             part = pl.ds(c * PART, PART)
             run = carried[2 * side, rows_c] + far_on * carried[2 * side + 1, rows_c]
             for n in range(ROW):
-                prefixes[side, order[n], part] = run
+                if side or order[n] % 2 == 0:
+                    prefixes[side, order[n], part] = run
                 if n < ROW - 1:
                     run = gathered[side, order[n], part] + factor[n] * run
-            for p in row_mates:
-                send(
-                    prefixes.at[side, p, part], state_in.at[side, chip, part],
-                    ret_s.at[0], ret_r.at[lax.rem(chip + CHIPS - p // 2, CHIPS)],
-                    seq_of(row, p),
-                )
-        state_in[side, chip] = prefixes[side, pos]
+            if side:
+                for p in row_mates:
+                    send(
+                        prefixes.at[1, p, part], state_in.at[1, chip, part], ret_s.at[0],
+                        ret_r.at[lax.rem(chip + CHIPS - p // 2, CHIPS)], seq_of(row, p),
+                    )
+            else:
+                for d in (2, 1, 3):
+                    t = lax.rem(chip + d, CHIPS)
+                    send(
+                        prefixes.at[0, 2 * t, part], landed.at[chip, part],
+                        ret_s.at[0], ret_r.at[CHIPS - d], seq_of(row, 2 * t + 1),
+                    )
+        if side:
+            state_in[1, chip] = prefixes[1, pos]
+        else:
+            landed[chip] = prefixes[0, 2 * chip]
 
     def next_head(side, d):
         head = lax.rem(chip + d, CHIPS)
-        if d:
+
+        @pl.when(core == 0)
+        def _():
             arrived(state_in.at[side, head], ret_r.at[d])
-        else:
-            @pl.when(core == 0)
-            def _():
-                arrived(state_in.at[side, head], ret_r.at[d])
+
+        @pl.when(core == 1)
+        def _():
+            if side:
+                if d:
+                    arrived(state_in.at[1, head], ret_r.at[d])
+            else:
+                if d:
+                    arrived(landed.at[head], ret_r.at[d])
+                send(
+                    landed.at[head], state_in.at[0, head],
+                    pass_s.at[0], ret_r.at[d], seq_of(row, pos - 1),
+                )
+                before = jnp.where(chip == 0, carried[0, 0:1], meta[lax.rem(pos + ROW - 2, ROW), 0:1, :])
+                factor = jnp.where(meta[pos - 1, 0:1, :] == before, lam_ref[pl.ds(head, 1)], 0.0)
+                state_in[0, head] = pair[head] + factor * landed[head]
         return head, pl.ds(pl.multiple_of(head * DIM, DIM), DIM)
 
     loads[2].wait()
@@ -327,6 +360,10 @@
     into_on = seg_col == prev_seg
     for h in range(heads):
         into_ref[h] = jnp.where(into_on, into_ref[h], 0.0)
+    @pl.when(core == 1)
+    def _():
+        arrived(pair, pair_r.at[0])
+
     squares = jnp.zeros((BLOCK, DIM), F32)
     crosses = jnp.zeros((BLOCK, DIM), F32)
     for d in (0, 1, 3, 2):
@@ -343,13 +380,13 @@
     for other in z_mates:
         send(z_own, z_all.at[z], z_s.at[0], z_r.at[0], {"seq": me, "head": other})
     z_all[z] = z_own[...]
+    step_tokens(4)
     for h in range(heads):
         start_gdy[h] = start_ref[h] * gdy_ref[h]
         start_att[h] = start_ref[h] * att_ref[h]
         q_turned[h] = q_ref[:, h * DIM:(h + 1) * DIM].T
     if zs > 1:
         arrived(z_all.at[pl.ds(0, zs - 1)], z_r.at[0])
-    step_tokens(4)
     both = z_all[0]
     for i in range(1, zs):
         both = both + z_all[i]
@@ -366,10 +403,11 @@
         cut = slice(h * DIM, (h + 1) * DIM)
         att = att_ref[h]
         back_ref[h] = gdy_ref[h] * inv - att * off
-        gr_own[h:h + 1] = jnp.sum(dy_ref[:, cut].astype(F32) * inv * att, axis=0, keepdims=True)
-    for p in row_mates:
-        send(gr_own, gr_all.at[pos], gr_s.at[0], gr_r.at[0], seq_of(row, p))
-    gr_all[pos] = gr_own[...]
+        gc_own[h:h + 1] = jnp.sum(dy_ref[:, cut].astype(F32) * inv * att, axis=0, keepdims=True)
+    step_tokens(5)
+    for r in col_mates:
+        send(gc_own, gc_all.at[row], gc_s.at[0], gc_r.at[0], seq_of(r, pos))
+    gc_all[row] = gc_own[...]
 
     def inner(h):
         cut = slice(h * DIM, (h + 1) * DIM)
@@ -386,15 +424,6 @@
     inner(0)
     inner(1)
     pl.when(core == 1)(lambda: scan_first(1))
-    step_tokens(5)
-    arrived(gr_all.at[row_others], gr_r.at[0])
-    total = gr_all[0]
-    for a in range(1, ROW):
-        total = total + gr_all[a]
-    gc_own[...] = total
-    gc_all[row] = total
-    for r in col_mates:
-        send(gc_own, gc_all.at[row], gc_s.at[0], gc_r.at[0], seq_of(r, pos))
     inner(2)
     pl.when(core == 1)(lambda: scan_second(1))
     next_seg = jnp.where(
@@ -405,8 +434,11 @@
     total = gc_all[0]
     for a in range(1, rows):
         total = total + gc_all[a]
-    for h in range(heads):
-        gg_ref[:, h * DIM:(h + 1) * DIM] = total[h:h + 1]
+    gr_own[...] = total
+    gr_all[pos] = total
+    for p in row_mates:
+        send(gr_own, gr_all.at[pos], gr_s.at[0], gr_r.at[0], seq_of(row, p))
+
     next_on = seg_col == next_seg
     for h in range(heads):
         next_ref[h] = jnp.where(next_on, next_ref[h], 0.0)
@@ -418,15 +450,23 @@
         dv = dv_acc[h] + weight * mm_split_right(k_ref[:, cut], grad, 1, 0)
         dk_ref[:, cut] = dk.astype(BF16)
         dv_ref[:, cut] = dv.astype(BF16)
+    arrived(gr_all.at[row_others], gr_r.at[0])
+    total = gr_all[0]
+    for a in range(1, ROW):
+        total = total + gr_all[a]
+    for h in range(heads):
+        gg_ref[:, h * DIM:(h + 1) * DIM] = total[h:h + 1]
     sent(meta.at[row_others], meta_s.at[0])
     @pl.when(core == 0)
     def _():
         sent(states, a2a_s.at[0])
+        sent(pair, pair_s.at[0])
 
     @pl.when(core == 1)
     def _():
         sent(states.at[:, pl.ds(0, CHIPS - 1)], a2a_s.at[0])
-        sent(prefixes.at[:, row_others], ret_s.at[0])
+        sent(prefixes.at[:, pl.ds(0, 5)], ret_s.at[0])
+        sent(landed, pass_s.at[0])
         moved = jnp.minimum(row, 2) + jnp.minimum(rows - 1 - row, 2)
         for n in (2, 3, 4):
             @pl.when(moved == n)
@@ -503,6 +543,8 @@
             pltpu.VMEM((HEAD_ROWS, DIM), F32), dma((1,)), dma((1,)),
             square, square, square, square, square, square,
             pltpu.VMEM((heads, DIM, DIM), BF16),
+            square, square, pltpu.VMEM((heads, DIM), F32),
+            dma((1,)), dma((1,)), dma((1,)),
         ],
         compiler_params=pltpu.CompilerParams(collective_id=0, has_side_effects=True),
     )(

time: 42.2 us -> 41.9 us (level)
  no operation moved by 1% of the time
where the time goes in v6:
time: 41.9 us; the launch traced here: 41.7 us
  Pallas kernels  41.1 us (98%)
  between operations  0.64 us (2%)
    pallas_call x1, Pallas kernels, local(): pl.pallas_call(functools.partial(kernel, rows, zs, heads), out_shape=(wid...  40.3 us

profile of v6, /device:TPU:17, one launch (start us, length us, event | category | flops | bytes accessed | tf_op | source)
XLA Modules:
  0.0 41.7 jit_solution(18238256590902889160)
XLA Ops:
  0.6 40.3 %shard_map.102 = (bf16[128,512]{1,0:T(8,128)(2,1)S(1)}, bf16[128,512]{1,0:T(8,128)(2,1)S(1)}, bf16[128,512]{1,0:T(8,128)(2,1)S(1)}, f32[1,512]{1,0:T(1,128)S(1)}) custom-call(bf16[128,512]{1,0:T(8,128)(2,1)} %q_hbm.1, bf16[128,512]{1,0:T(8,128)(2,1)} %k_hbm.1, bf16[128,512]{1,0:T(8,128)(2,1)} %v_hbm.1, bf16[128,512]{1,0:T(8,128)(2,1)} %dy_hbm.1, ...), custom_call_target="tpu_custom_call" | custom-call | tf_op jit(solution)/shard_map/pallas_call | solution.py:510
  40.9 0.8 %shard_map.103 = (bf16[128,512]{1,0:T(8,128)(2,1)}, bf16[128,512]{1,0:T(8,128)(2,1)}, bf16[128,512]{1,0:T(8,128)(2,1)}, f32[1,512]{1,0:T(1,128)}) custom-call(bf16[128,512]{1,0:T(8,128)(2,1)S(1)} %get-tuple-element.12.refs_0_, bf16[128,512]{1,0:T(8,128)(2,1)S(1)} %get-tuple-element.13.refs_1_, bf16[128,512]{1,0:T(8,128)(2,1)S(1)} %get-tuple-element.14.refs_2_, ...), custom_call_target="tpu_custom_call" | custom-call | tf_op jit(solution)/shard_map/pallas_call | solution.py:555

commit v7 on v6

--- a/solution.py
+++ b/solution.py
@@ -45,12 +45,12 @@
     rows, zs, heads,
     q_hbm, k_hbm, v_hbm, dy_hbm, seg_hbm, span_hbm, gain_hbm,
     dq_ref, dk_ref, dv_ref, gg_ref,
-    q_ref, k_ref, v_ref, dy_ref, seg_ref, span_ref, gain_ref,
+    kv_ref, qd_ref, seg_ref, span_ref, gain_ref,
     meta_own, meta, states, gathered, totals, carried, prefixes, state_in,
     z_own, z_all, gr_own, gr_all, gc_own, gc_all,
     att_ref, back_ref, w_ref, dk_acc, dv_acc, qk_ref,
-    in_sem, meta_s, meta_r, a2a_s, a2a_r, col_s, col_r, ret_s, ret_r,
-    z_s, z_r, gr_s, gr_r, gc_s, gc_r, tokens, edge, edge_s, edge_r,
+    in_sem, small_s, meta_r, a2a_s, a2a_r, col_s, col_r, ret_s, ret_r,
+    z_r, gr_r, gc_r, tokens, edge, edge_r,
     into_ref, next_ref, start_ref, gdy_ref, start_gdy, start_att, q_turned,
     pair, landed, lam_ref, pair_s, pair_r, pass_s,
 ):
@@ -60,18 +60,16 @@
     pos = lax.rem(me, ROW)
     chip, core = pos // 2, lax.rem(pos, 2)
     features = float(zs * heads * DIM)
-
-    loads = [
-        pltpu.make_async_copy(src, dst, in_sem.at[i])
-        for i, (src, dst) in enumerate(
-            (
-                (k_hbm, k_ref), (v_hbm, v_ref), (q_hbm, q_ref), (dy_hbm, dy_ref),
-                (seg_hbm, seg_ref), (span_hbm, span_ref), (gain_hbm, gain_ref),
-            )
-        )
-    ]
-    for i in (4, 5, 0, 1, 2, 3, 6):
-        loads[i].start()
+    k_ref, v_ref, q_ref, dy_ref = kv_ref.at[0], kv_ref.at[1], qd_ref.at[0], qd_ref.at[1]
+
+    def load(src, dst, i):
+        return pltpu.make_async_copy(src, dst, in_sem.at[i])
+
+    for src, dst, i in (
+        (seg_hbm, seg_ref, 2), (span_hbm, span_ref, 3), (k_hbm, k_ref, 0), (v_hbm, v_ref, 0),
+        (q_hbm, q_ref, 1), (dy_hbm, dy_ref, 1), (gain_hbm, gain_ref, 4),
+    ):
+        load(src, dst, i).start()
 
     def seq_of(r, p):
         return {"seq": r * ROW + p, "head": z}
@@ -141,8 +139,8 @@
         remote(buffer, buffer, ss, ss, seq_of(row, row_mates[0])).wait_send()
 
     row_others = pl.ds(0, ROW - 1)
-    loads[4].wait()
-    loads[5].wait()
+    load(seg_hbm, seg_ref, 2).wait()
+    load(span_hbm, span_ref, 3).wait()
 
     t_col = lax.broadcasted_iota(jnp.int32, (BLOCK, DIM), 0).astype(F32)
     s_row = lax.broadcasted_iota(jnp.int32, (BLOCK, DIM), 1).astype(F32)
@@ -166,8 +164,7 @@
         att_ref[h] = jnp.where(
             seg_col == last_own, jnp.exp((t_col - (BLOCK - 1.0)) * inverse[h]), 0.0
         )
-    loads[0].wait()
-    loads[1].wait()
+    load(kv_ref, kv_ref, 0).wait()
     for h in range(heads):
         cut = slice(h * DIM, (h + 1) * DIM)
         local = mm_split_right(
@@ -213,7 +210,7 @@
         return order, [meta[a, side:side + 1, :] for a in order]
 
     for p in row_mates:
-        send(meta_own, meta.at[pos], meta_s.at[0], meta_r.at[0], seq_of(row, p))
+        send(meta_own, meta.at[pos], small_s.at[0], meta_r.at[0], seq_of(row, p))
     scatter(0)
 
     def before_of(side):
@@ -267,7 +264,7 @@
                     @pl.when(pos == 1)
                     def _():
                         send(carried.at[0, pl.ds(0, HEAD_ROWS)], edge,
-                             edge_s.at[0], edge_r.at[0], seq_of(row, pos - 1))
+                             small_s.at[0], edge_r.at[0], seq_of(row, pos - 1))
                 near_seg = carried[2 * side, 0:1]
                 far_seg = carried[2 * side + 1, 0:1]
                 far_on = jnp.where(far_seg == near_seg, lam_row, 0.0)
@@ -323,7 +320,7 @@
                 state_in[0, head] = pair[head] + factor * landed[head]
         return head, pl.ds(pl.multiple_of(head * DIM, DIM), DIM)
 
-    loads[2].wait()
+    load(qd_ref, qd_ref, 1).wait()
     causal = t_col >= s_row
     same = seg_col == seg_tile
     keep = jnp.logical_and(causal, same)
@@ -339,8 +336,7 @@
         next_ref[h] = jnp.exp((t_col - float(BLOCK)) * inverse[h])
         start_ref[h] = jnp.where(seg_col == first_own, jnp.exp(-t_col * inverse[h]), 0.0)
 
-    loads[3].wait()
-    loads[6].wait()
+    load(gain_hbm, gain_ref, 4).wait()
     for h in range(heads):
         cut = slice(h * DIM, (h + 1) * DIM)
         gdy_ref[h] = gain_ref[:, cut] * dy_ref[:, cut].astype(F32)
@@ -378,7 +374,7 @@
     z_own[0:1] = square_row
     z_own[1:2] = cross_row
     for other in z_mates:
-        send(z_own, z_all.at[z], z_s.at[0], z_r.at[0], {"seq": me, "head": other})
+        send(z_own, z_all.at[z], small_s.at[0], z_r.at[0], {"seq": me, "head": other})
     z_all[z] = z_own[...]
     step_tokens(4)
     for h in range(heads):
@@ -406,7 +402,7 @@
         gc_own[h:h + 1] = jnp.sum(dy_ref[:, cut].astype(F32) * inv * att, axis=0, keepdims=True)
     step_tokens(5)
     for r in col_mates:
-        send(gc_own, gc_all.at[row], gc_s.at[0], gc_r.at[0], seq_of(r, pos))
+        send(gc_own, gc_all.at[row], small_s.at[0], gc_r.at[0], seq_of(r, pos))
     gc_all[row] = gc_own[...]
 
     def inner(h):
@@ -437,7 +433,7 @@
     gr_own[...] = total
     gr_all[pos] = total
     for p in row_mates:
-        send(gr_own, gr_all.at[pos], gr_s.at[0], gr_r.at[0], seq_of(row, p))
+        send(gr_own, gr_all.at[pos], small_s.at[0], gr_r.at[0], seq_of(row, p))
 
     next_on = seg_col == next_seg
     for h in range(heads):
@@ -456,7 +452,11 @@
         total = total + gr_all[a]
     for h in range(heads):
         gg_ref[:, h * DIM:(h + 1) * DIM] = total[h:h + 1]
-    sent(meta.at[row_others], meta_s.at[0])
+    few = 2 * (ROW - 1 + zs - 1) + heads * (ROW - 1 + rows - 1)
+    for at_edge in (True, False):
+        @pl.when((pos == 1) == at_edge)
+        def _():
+            sent(totals.at[0, pl.ds(0, few + HEAD_ROWS * at_edge)], small_s.at[0])
     @pl.when(core == 0)
     def _():
         sent(states, a2a_s.at[0])
@@ -473,25 +473,18 @@
             def _():
                 sent(carried.at[pl.ds(0, n)], col_s.at[0])
 
-    @pl.when(pos == 1)
-    def _():
-        sent(edge, edge_s.at[0])
-
-    if zs > 1:
-        sent(z_all.at[pl.ds(0, zs - 1)], z_s.at[0])
-    sent(gr_all.at[row_others], gr_s.at[0])
-    sent(gc_all.at[pl.ds(0, rows - 1)], gc_s.at[0])
-
 
 def store(*refs):
     count = (len(refs) - 1) // 2
-    copies = [
-        pltpu.make_async_copy(refs[i], refs[count + i], refs[-1].at[i]) for i in range(count)
-    ]
-    for copy in copies:
-        copy.start()
-    for copy in copies:
-        copy.wait()
+    for i in range(count):
+        tall = refs[i].shape[0]
+        for at in range(0, tall, 32):
+            part = pl.ds(at, min(32, tall))
+            pltpu.make_async_copy(
+                refs[i].at[part], refs[count + i].at[part], refs[-1].at[i]
+            ).start()
+    for i in range(count):
+        pltpu.make_async_copy(refs[i], refs[count + i], refs[-1].at[i]).wait()
 
 
 def local(queries, key_rows, value_rows, segment_ids, decay_span, norm_gain, out_grad):
@@ -502,6 +495,7 @@
     far = pl.BlockSpec(memory_space=pl.ANY)
     near = pl.BlockSpec(memory_space=pltpu.VMEM)
     wide = pltpu.VMEM((BLOCK, width), BF16)
+    pair = pltpu.VMEM((2, BLOCK, width), BF16)
     square = pltpu.VMEM((heads, DIM, DIM), F32)
     pieces = pltpu.VMEM((2, ROW, DIM, DIM), F32)
     per_head = pltpu.VMEM((2, heads, DIM, DIM), F32)
@@ -513,7 +507,7 @@
         in_specs=[far] * 7,
         out_specs=(near,) * 4,
         scratch_shapes=[
-            wide, wide, wide, wide,
+            pair, pair,
             pltpu.VMEM((1, BLOCK), jnp.int32), pltpu.SMEM((heads,), F32), kept,
             pltpu.VMEM((2, DIM), F32),
             pltpu.VMEM((ROW, 2, DIM), F32),
@@ -531,16 +525,14 @@
             pltpu.VMEM((rows, heads, DIM), F32),
             square, square, square, square, square,
             pltpu.VMEM((heads, 2, DIM, DIM), BF16),
-            dma((7,)),
+            dma((5,)),
             dma((1,)), dma((1,)),
             dma((1,)), dma((CHUNKS,)),
             dma((1,)), dma((2, CHUNKS)),
             dma((1,)), dma((CHIPS,)),
-            dma((1,)), dma((1,)),
-            dma((1,)), dma((1,)),
-            dma((1,)), dma((1,)),
+            dma((1,)), dma((1,)), dma((1,)),
             pltpu.SemaphoreType.REGULAR((2, 2)),
-            pltpu.VMEM((HEAD_ROWS, DIM), F32), dma((1,)), dma((1,)),
+            pltpu.VMEM((HEAD_ROWS, DIM), F32), dma((1,)),
             square, square, square, square, square, square,
             pltpu.VMEM((heads, DIM, DIM), BF16),
             square, square, pltpu.VMEM((heads, DIM), F32),

time: 41.9 us -> 41.8 us (level)
  no operation moved by 1% of the time
where the time goes in v7:
time: 41.8 us; the launch traced here: 41.7 us
  Pallas kernels  41 us (98%)
  between operations  0.64 us (2%)
    pallas_call x1, Pallas kernels, local(): pl.pallas_call(functools.partial(kernel, rows, zs, heads), out_shape=(wid...  40.3 us

profile of v7, /device:TPU:17, one launch (start us, length us, event | category | flops | bytes accessed | tf_op | source)
XLA Modules:
  0.0 41.7 jit_solution(4733717875244490597)
XLA Ops:
  0.6 40.3 %shard_map.102 = (bf16[128,512]{1,0:T(8,128)(2,1)S(1)}, bf16[128,512]{1,0:T(8,128)(2,1)S(1)}, bf16[128,512]{1,0:T(8,128)(2,1)S(1)}, f32[1,512]{1,0:T(1,128)S(1)}) custom-call(bf16[128,512]{1,0:T(8,128)(2,1)} %q_hbm.1, bf16[128,512]{1,0:T(8,128)(2,1)} %k_hbm.1, bf16[128,512]{1,0:T(8,128)(2,1)} %v_hbm.1, bf16[128,512]{1,0:T(8,128)(2,1)} %dy_hbm.1, ...), custom_call_target="tpu_custom_call" | custom-call | tf_op jit(solution)/shard_map/pallas_call | solution.py:504
  40.9 0.8 %shard_map.103 = (bf16[128,512]{1,0:T(8,128)(2,1)}, bf16[128,512]{1,0:T(8,128)(2,1)}, bf16[128,512]{1,0:T(8,128)(2,1)}, f32[1,512]{1,0:T(1,128)}) custom-call(bf16[128,512]{1,0:T(8,128)(2,1)S(1)} %get-tuple-element.12.refs_0_, bf16[128,512]{1,0:T(8,128)(2,1)S(1)} %get-tuple-element.13.refs_1_, bf16[128,512]{1,0:T(8,128)(2,1)S(1)} %get-tuple-element.14.refs_2_, ...), custom_call_target="tpu_custom_call" | custom-call | tf_op jit(solution)/shard_map/pallas_call | solution.py:547
